TPU v7x, 256 devices: a whole 4x4x8 slice. The times are simulated.
256 devices in a mesh: dp: 2 (over core), seq: 16 (over y, x), head: 8 (over z).
Axes of the slice: x: 4, y: 4, z: 8, core: 2. Of those that a mesh axis runs over, the one named last changes fastest.
Arguments:
- query_rows: bfloat16 [2, 8192, 8192], P('dp', 'seq', 'head'), may hold values from -1.796875 to 1.796875
- key_rows: bfloat16 [2, 8192, 8192], P('dp', 'seq', 'head'), may hold values from -1.796875 to 1.796875
- value_rows: bfloat16 [2, 8192, 8192], P('dp', 'seq', 'head'), may hold values from -6 to 6
- norm_gain: float32 [8192], P('head'), may hold values from 0.1 to 1.9
- cotangent: bfloat16 [2, 8192, 8192], P('dp', 'seq', 'head'), may hold values from -10 to 10
- loss_mask: int32 [2, 8192], P('dp', 'seq'), may hold values 0 or 1
- importance: float32 [2, 8192], P('dp', 'seq'), may hold values from 0.5 to 2
- advantage: float32 [2], P('dp'), may hold values from -3 to 3
- lengths: int32 [2], P('dp'), may hold values from 2048 to 8192, as said below
- decay_index: int32 [64], P('head'), may hold values from 0 to 11
Outputs:
- mixed: bfloat16 [2, 8192, 8192], P('dp', 'seq', 'head')
- query_grad: bfloat16 [2, 8192, 8192], P('dp', 'seq', 'head')
- key_grad: bfloat16 [2, 8192, 8192], P('dp', 'seq', 'head')
- value_grad: bfloat16 [2, 8192, 8192], P('dp', 'seq', 'head')
- gain_grad: float32 [8192], P('head')
Inputs may be any that keep to these rules, and one draw needn't show every extreme that they name: `lengths`: at least one response has length 8192.
All inputs are finite; a program needn't handle non-finite values. No bound on the sum of `loss_mask` on one device may be relied on, other than what follows from the above.
Results may differ from a plain program's by a relative error of at most 0.0063.
Values sent between devices are 32-bit elements; how exact they have to be, the bound alone decides.
No kernel may reach another device: no remote copies, remote signals or barrier semaphores. Data moves between devices by JAX's collectives and lax.ppermute only.
A program may use at most 128 MiB of HBM per device.

v0:
```python
import jax
import jax.numpy as jnp
from jax import lax
from jax.sharding import Mesh
from jax.sharding import PartitionSpec as P

SEQ = ("seq_0", "seq_1")
DP_SEQ = ("dp", "seq_0", "seq_1")


clip_high = 1.28
epsilon = 1e-06


def filled_with(value, identity):
    return jax.tree.map(
        lambda a, e: jnp.broadcast_to(jnp.asarray(e, a.dtype), a.shape), value, identity
    )


def prefix_by_axis(value, axes, combine, identity, reverse):
    before = start = filled_with(value, identity)
    running = value
    for axis in reversed(axes):
        count, place = (lax.axis_size(axis), lax.axis_index(axis))
        pieces = jax.tree.map(lambda part: lax.all_gather(part, axis), running)
        inside, running = (start, start)
        for k in reversed(range(count)) if reverse else range(count):
            passed = k > place if reverse else k < place
            running = combine(running, jax.tree.map(lambda part: part[k], pieces))
            inside = jax.tree.map(lambda new, old: jnp.where(passed, new, old), running, inside)
        before = combine(inside, before)
    return before


def sent_to_all(value, axis):
    count = lax.axis_size(axis)
    return lax.all_to_all(
        jnp.broadcast_to(value[None], (count, *value.shape)), axis, 0, 0, tiled=True
    )


def taken_together(value, axis):
    return sent_to_all(value, axis).sum(axis=0)


def together(arrays, axis):
    ends = [0]
    for a in arrays:
        ends.append(ends[-1] + a.size)
    running = taken_together(jnp.concatenate([a.ravel() for a in arrays]), axis)
    return tuple((running[b:e].reshape(a.shape) for a, b, e in zip(arrays, ends, ends[1:])))


def on_device(
    query_rows,
    key_rows,
    value_rows,
    norm_gain,
    cotangent,
    loss_mask,
    importance,
    advantage,
    lengths,
    decay_index,
):
    batches, slab_len, features = query_rows.shape
    head_count = decay_index.shape[0]
    per_head = features // head_count
    seq_count = lax.axis_size(SEQ)
    seq_place = lax.axis_index(SEQ)
    decay_rate = 16.0 / (slab_len * jnp.exp2(decay_index.astype(jnp.float32)))
    query_heads = query_rows.reshape(batches, slab_len, head_count, per_head)
    key_heads = key_rows.reshape(batches, slab_len, head_count, per_head)
    value_heads = value_rows.reshape(batches, slab_len, head_count, per_head)
    offsets = jnp.arange(slab_len, dtype=jnp.float32)
    lagged = offsets[:, None] - offsets[None, :]
    within = jnp.where(
        lagged[None] >= 0,
        jnp.exp2(-decay_rate[:, None, None] * jnp.maximum(lagged, 0.0)[None]),
        0.0,
    )
    from_start = jnp.exp2(-decay_rate[None, :] * (offsets + 1.0)[:, None])
    to_next = jnp.exp2(-decay_rate[None, :] * (slab_len - offsets)[:, None])
    to_end = jnp.exp2(-decay_rate[None, :] * (slab_len - 1.0 - offsets)[:, None])
    from_begin = jnp.exp2(-decay_rate[None, :] * offsets[:, None])
    block_decay = jnp.exp2(-decay_rate * slab_len)
    scores = jnp.einsum(
        "bthd,bshd->bhts", query_heads, key_heads, preferred_element_type=jnp.float32
    )
    score_half = (scores * within[None]).astype(jnp.bfloat16)
    local_out = jnp.einsum(
        "bhts,bshd->bthd", score_half, value_heads, preferred_element_type=jnp.float32
    )
    key_decayed = (key_heads.astype(jnp.float32) * to_end[None, :, :, None]).astype(jnp.bfloat16)
    state_local = jnp.einsum(
        "bthd,bthe->bhde", key_decayed, value_heads, preferred_element_type=jnp.float32
    )

    def combine_states(earlier, later):
        return (earlier[0] * later[0], later[1] + later[0][None, :, None, None] * earlier[1])

    identity_pair = (jnp.ones_like(block_decay), jnp.zeros_like(state_local))
    state_in = prefix_by_axis(
        (block_decay, state_local), SEQ, combine_states, identity_pair, False
    )[1]
    state_half = state_in.astype(jnp.bfloat16)
    carried = jnp.einsum(
        "bthd,bhde->bthe", query_heads, state_half, preferred_element_type=jnp.float32
    )
    outputs_flat = (local_out + carried * from_start[None, :, :, None]).reshape(
        batches, slab_len, features
    )
    positions = seq_place * slab_len + jnp.arange(slab_len, dtype=jnp.int32)
    in_length = (positions[None, :] < lengths[:, None]).astype(jnp.float32)
    token_weight = loss_mask.astype(jnp.float32) * in_length * jnp.minimum(importance, clip_high)
    token_weight = (
        token_weight
        * advantage[:, None]
        * (float(slab_len * seq_count) / lengths.astype(jnp.float32))[:, None]
    )
    grad_y = cotangent.astype(jnp.float32) * token_weight[..., None]
    grad_n = grad_y * norm_gain
    statistics = together(
        (jnp.sum(outputs_flat * outputs_flat, -1), jnp.sum(grad_n * outputs_flat, -1)), "head"
    )
    total_features = features * lax.axis_size("head")
    inverse = lax.rsqrt(statistics[0] / total_features + epsilon)
    normed = outputs_flat * inverse[..., None]
    mixed = (normed * norm_gain).astype(jnp.bfloat16)
    mean_term = statistics[1] * inverse / total_features
    grad_out = (inverse[..., None] * (grad_n - normed * mean_term[..., None])).astype(jnp.bfloat16)
    gain_grad = taken_together(jnp.sum(grad_y * normed, axis=(0, 1)), DP_SEQ)
    grad_heads = grad_out.reshape(batches, slab_len, head_count, per_head)
    dscore = jnp.einsum(
        "bthe,bshe->bhts", grad_heads, value_heads, preferred_element_type=jnp.float32
    )
    dscore = (dscore * within[None]).astype(jnp.bfloat16)
    query_decayed = (query_heads.astype(jnp.float32) * from_begin[None, :, :, None]).astype(
        jnp.bfloat16
    )
    return_local = jnp.einsum(
        "bthd,bthe->bhde", query_decayed, grad_heads, preferred_element_type=jnp.float32
    )
    return_identity = (jnp.ones_like(block_decay), jnp.zeros_like(return_local))
    return_in = prefix_by_axis(
        (block_decay, return_local), SEQ, combine_states, return_identity, True
    )[1]
    return_half = return_in.astype(jnp.bfloat16)
    query_grad = jnp.einsum(
        "bhts,bshd->bthd", dscore, key_heads, preferred_element_type=jnp.float32
    )
    query_grad = (
        query_grad
        + jnp.einsum("bthe,bhde->bthd", grad_heads, state_half, preferred_element_type=jnp.float32)
        * from_start[None, :, :, None]
    )
    key_grad = jnp.einsum(
        "bhts,bthd->bshd", dscore, query_heads, preferred_element_type=jnp.float32
    )
    key_grad = (
        key_grad
        + jnp.einsum(
            "bthe,bhde->bthd", value_heads, return_half, preferred_element_type=jnp.float32
        )
        * to_next[None, :, :, None]
    )
    value_grad = jnp.einsum(
        "bhts,bthe->bshe", score_half, grad_heads, preferred_element_type=jnp.float32
    )
    value_grad = (
        value_grad
        + jnp.einsum("bthd,bhde->bthe", key_heads, return_half, preferred_element_type=jnp.float32)
        * to_next[None, :, :, None]
    )
    query_grad = query_grad.reshape(batches, slab_len, features).astype(jnp.bfloat16)
    key_grad = key_grad.reshape(batches, slab_len, features).astype(jnp.bfloat16)
    value_grad = value_grad.reshape(batches, slab_len, features).astype(jnp.bfloat16)
    return (mixed, query_grad, key_grad, value_grad, gain_grad)


def solution(mesh):
    split = Mesh(
        mesh.devices.reshape(mesh.shape["dp"], 4, 4, mesh.shape["head"]),
        ("dp", "seq_0", "seq_1", "head"),
    )
    return jax.shard_map(
        on_device,
        mesh=split,
        in_specs=(
            P("dp", SEQ, "head"),
            P("dp", SEQ, "head"),
            P("dp", SEQ, "head"),
            P("head"),
            P("dp", SEQ, "head"),
            P("dp", SEQ),
            P("dp", SEQ),
            P("dp"),
            P("dp"),
            P("head"),
        ),
        out_specs=(
            P("dp", SEQ, "head"),
            P("dp", SEQ, "head"),
            P("dp", SEQ, "head"),
            P("dp", SEQ, "head"),
            P("head"),
        ),
        check_vma=False,
    )
```

profile of v0, /device:TPU:2, one launch (start us, length us, event | category | flops | bytes accessed | tf_op | source)
XLA Modules:
  0.0 204.9 jit_solution(3679143968662598284)
XLA Ops:
  7.2 0.0 all-gather.14.cloned.1.call-start
  7.2 1.5 copy.117
  8.8 0.0 copy-start.37
  8.8 0.0 copy-start.36
  8.8 0.7 copy.87
  9.5 1.9 copy.118
  11.3 0.0 copy-start.4
  11.4 0.7 dynamic-slice
  12.7 0.1 exponential_dynamic-update-slice_fusion
  12.8 0.1 multiply_exponential_fusion
  13.0 1.3 fusion.8
  14.2 0.0 all-gather.14.cloned.1.call-update
  14.3 0.0 all-gather.10.cloned.1.call-start
  14.3 10.0 %all-reduce = f32[32]{0:T(128)S(1)} all-reduce(f32[32]{0:T(128)S(1)} %get-tuple-element.25), channel_id=3, replica_groups=mesh['dp'=2,'seq_0'=4,'seq_1'=4,'head'=8] {'seq_1'}, use_global_device_ids=true, to_apply=%add | all-reduce | flops 32 | bytes 256
  24.3 0.1 fusion.57
  24.4 0.7 broadcast_select_fusion.3
  25.1 24.7 %all-gather.14.cloned.1.call-done = f32[32,128,128]{2,1,0:T(8,128)} async-done(((f32[8,128,128]{2,1,0:T(8,128)}), f32[32,128,128]{2,1,0:T(8,128)}) %all-gather.14.cloned.1.call-update) | async-done | bytes 2097168 | tf_op jit(solution)/shard_map/all_gather | solution.py:26
  49.8 2.5 %fusion.49 = f32[1,1,8,128,128]{4,3,2,1,0:T(8,128)} fusion(f32[32,128,128]{2,1,0:T(8,128)} %all-gather.14.cloned.1.call-done, f32[8]{0:T(128)S(1)} %get-tuple-element.46, f32[8]{0:T(128)S(1)} %get-tuple-element.53, f32[8]{0:T(128)S(1)} %get-tuple-element.48, f32[8]{0:T(128)S(1)} %get-tuple-element.52), kind=kLoop, calls=%fused_computation.75 | loop fusion | flops 917504 | bytes 2621568 | tf_op jit(solution)/shard_map/add | solution.py:101
  52.3 0.0 all-gather.10.cloned.1.call-update
  52.4 0.0 all-gather.16.cloned.1.call-start
  52.4 0.6 fusion.56
  53.0 9.6 %all-gather.3 = f32[4,1,8]{2,1,0:T(1,128)S(1)} all-gather(f32[1,1,8]{2,1,0:T(1,128)S(1)} %get-tuple-element.50), channel_id=1, replica_groups=mesh['dp'=2,'seq_0'=4,'seq_1'=4,'head'=8] {'seq_0'}, dimensions={0}, use_global_device_ids=true | all-gather | bytes 160 | tf_op jit(solution)/shard_map/all_gather | solution.py:26
  63.9 1.5 copy.115
  65.5 0.3 fusion.13
  65.8 0.2 fusion.12
  66.0 0.0 copy-start.11
  66.0 3.1 %multiply_convert_fusion.1 = bf16[8,512,512]{2,1,0:T(8,128)(2,1)S(1)} fusion(f32[512,512]{1,0:T(8,128)S(1)} %fusion.12, f32[8]{0:T(128)S(1)} %get-tuple-element.26, pred[512,512]{1,0:T(8,128)(4,1)S(1)} %fusion.13, bf16[512,8,128]{0,2,1:T(8,128)(2,1)S(1)} %bitcast.241, bf16[512,8,128]{2,1,0:T(8,128)(2,1)S(1)} %bitcast.246), kind=kOutput, calls=%fused_computation.1 | convolution fusion | flops 547356672 | bytes 7602208 | tf_op jit(solution)/shard_map/bthd,bshd->bhts/dot_general | solution.py:88
  69.2 2.0 copy-done
  71.2 2.8 %fusion.16 = f32[8,512,128]{1,2,0:T(8,128)} fusion(bf16[8,512,512]{2,1,0:T(8,128)(2,1)S(1)} %multiply_convert_fusion.1, bf16[512,8,128]{2,1,0:T(8,128)(2,1)S(1)} %bitcast.249), kind=kOutput, calls=%fused_computation.32 | convolution fusion | flops 536870912 | bytes 7340032 | tf_op jit(solution)/shard_map/bhts,bshd->bthd/dot_general | solution.py:92
  74.0 12.9 %all-gather.10.cloned.1.call-done = f32[4,1,8,128,128]{4,3,2,1,0:T(8,128)} async-done(((f32[1,1,8,128,128]{4,3,2,1,0:T(8,128)}), f32[4,1,8,128,128]{4,3,2,1,0:T(8,128)}) %all-gather.10.cloned.1.call-update) | async-done | bytes 2097168 | tf_op jit(solution)/shard_map/all_gather | solution.py:26
  86.9 3.0 %fusion.37 = bf16[8,128,128]{2,1,0:T(8,128)(2,1)S(1)} fusion(f32[4,1,8,128,128]{4,3,2,1,0:T(8,128)} %all-gather.10.cloned.1.call-done, f32[32,128,128]{2,1,0:T(8,128)} %all-gather.14.cloned.1.call-done, f32[8]{0:T(128)S(1)} %get-tuple-element.53, f32[8]{0:T(128)S(1)} %get-tuple-element.48, f32[8]{0:T(128)S(1)} %get-tuple-element.52, ...), kind=kLoop, calls=%fused_computation.61 | loop fusion | flops 3276800 | bytes 4456744 | tf_op jit(solution)/shard_map/convert_element_type | solution.py:107
  90.0 1.9 multiply_reduce_fusion.2
  91.9 1.9 copy.93
  93.8 1.7 multiply_reduce_fusion.1
  95.6 14.8 %all_to_all.12 = f32[8,1,1024]{2,1,0:T(1,128)S(1)} all-to-all(f32[8,1,1024]{2,1,0:T(1,128)S(1)} %broadcast_in_dim.18), channel_id=1, replica_groups=mesh['dp'=2,'seq_0'=4,'seq_1'=4,'head'=8] {'head'}, dimensions={0} | all-to-all | bytes 65536 | tf_op jit(solution)/shard_map/all_to_all | solution.py:38
  110.5 3.4 %multiply_reduce_fusion = (f32[1024]{0:T(1024)S(1)}, bf16[1,512,1024]{2,1,0:T(8,128)(2,1)}, bf16[1,512,1024]{2,1,0:T(8,128)(2,1)}) fusion(bf16[1,512,1024]{2,1,0:T(8,128)(2,1)} %param.14, f32[1,512,1024]{2,1,0:T(8,128)S(1)} %copy.93, f32[512]{0:T(512)S(1)} %get-tuple-element.31, f32[512]{0:T(512)S(1)} %bitcast.259, f32[512]{0:T(512)S(1)} %get-tuple-element.30, ...), kind=kLoop, calls=%fused_computation.14 | loop fusion | flops 6290432 | bytes 5257216 | tf_op jit(solution)/shard_map/reduce_sum | solution.py:133
  113.9 1.5 copy.116
  115.4 1.2 fusion.9
  116.6 0.0 all-gather.16.cloned.1.call-update
  116.6 0.0 all-gather.12.cloned.1.call-start
  116.7 27.4 %all-gather.16.cloned.1.call-done = f32[32,128,128]{2,1,0:T(8,128)} async-done(((f32[8,128,128]{2,1,0:T(8,128)}), f32[32,128,128]{2,1,0:T(8,128)}) %all-gather.16.cloned.1.call-update) | async-done | bytes 2097168 | tf_op jit(solution)/shard_map/all_gather | solution.py:26
  144.1 2.6 %fusion.43 = f32[1,1,8,128,128]{4,3,2,1,0:T(8,128)} fusion(f32[32,128,128]{2,1,0:T(8,128)} %all-gather.16.cloned.1.call-done, f32[8]{0:T(128)S(1)} %get-tuple-element.45, f32[8]{0:T(128)S(1)} %get-tuple-element.51, f32[8]{0:T(128)S(1)} %get-tuple-element.53, f32[8]{0:T(128)S(1)} %get-tuple-element.48), kind=kLoop, calls=%fused_computation.68 | loop fusion | flops 917504 | bytes 2621568 | tf_op jit(solution)/shard_map/add | solution.py:101
  146.7 0.0 all-gather.12.cloned.1.call-update
  146.7 9.7 %all-gather.4 = f32[4,1,8]{2,1,0:T(1,128)S(1)} all-gather(f32[1,1,8]{2,1,0:T(1,128)S(1)} %copy-done.33), channel_id=1, replica_groups=mesh['dp'=2,'seq_0'=4,'seq_1'=4,'head'=8] {'seq_0'}, dimensions={0}, use_global_device_ids=true | all-gather | bytes 160 | tf_op jit(solution)/shard_map/all_gather | solution.py:26
  156.3 0.6 slice_bitcast_fusion.10
  156.9 0.7 broadcast_in_dim.19
  157.6 5.0 %all-to-all-start.1 = ((f32[32,1,1024]{2,1,0:T(1,128)}), f32[32,1,1024]{2,1,0:T(1,128)S(1)}, u32[]{:S(2)}, u32[]{:S(2)}) async-start(f32[32,1,1024]{2,1,0:T(1,128)} %broadcast_in_dim.19), calls=%async_computation.1 | async-start | bytes 262144 | tf_op jit(solution)/shard_map/all_to_all | solution.py:38
  162.6 0.0 copy-start.5
  162.7 0.0 copy-start.12
  162.7 4.4 %fusion.59 = f32[8,128,512]{2,1,0:T(8,128)} fusion(bf16[512,8,128]{0,2,1:T(8,128)(2,1)S(1)} %bitcast.238, bf16[8,512,512]{2,1,0:T(8,128)(2,1)} %copy-done), kind=kOutput, calls=%fused_computation.121 | convolution fusion | flops 536870912 | bytes 7340032 | tf_op jit(solution)/shard_map/bhts,bthe->bshe/dot_general | solution.py:168
  167.1 3.1 %multiply_convert_fusion = bf16[8,512,512]{2,1,0:T(8,128)(2,1)S(1)} fusion(f32[512,512]{1,0:T(8,128)S(1)} %copy-done.12, f32[8]{0:T(128)S(1)} %copy-done.28, pred[512,512]{1,0:T(8,128)(4,1)S(1)} %copy-done.14, bf16[512,8,128]{0,2,1:T(8,128)(2,1)S(1)} %bitcast.239, bf16[512,8,128]{2,1,0:T(8,128)(2,1)S(1)} %bitcast.250), kind=kOutput, calls=%fused_computation | convolution fusion | flops 547356672 | bytes 7602208 | tf_op jit(solution)/shard_map/bthe,bshe->bhts/dot_general | solution.py:135
  170.3 1.5 fusion.58
  171.7 0.5 copy-done.1
  172.2 1.4 fusion.5
  173.7 2.3 %copy.106 = bf16[1,512,1024]{2,1,0:T(8,128)(2,1)} copy(bf16[1,512,1024]{1,2,0:T(8,128)(2,1)} %bitcast.253) | data formatting | bytes 2097152
  176.0 0.7 reduce_sum.49
  176.7 6.0 %all-gather.12.cloned.1.call-done = f32[4,1,8,128,128]{4,3,2,1,0:T(8,128)} async-done(((f32[1,1,8,128,128]{4,3,2,1,0:T(8,128)}), f32[4,1,8,128,128]{4,3,2,1,0:T(8,128)}) %all-gather.12.cloned.1.call-update) | async-done | bytes 2097168 | tf_op jit(solution)/shard_map/all_gather | solution.py:26
  182.7 2.9 %fusion.29 = bf16[8,128,128]{2,1,0:T(8,128)(2,1)S(1)} fusion(f32[4,1,8,128,128]{4,3,2,1,0:T(8,128)} %all-gather.12.cloned.1.call-done, f32[32,128,128]{2,1,0:T(8,128)} %all-gather.16.cloned.1.call-done, f32[8]{0:T(128)S(1)} %copy-done.21, f32[8]{0:T(128)S(1)} %copy-done.19, f32[8]{0:T(128)S(1)} %copy-done.32, f32[8]{0:T(128)S(1)} %copy-done.30, ...), kind=kLoop, calls=%fused_computation.49 | loop fusion | flops 3276800 | bytes 4456744 | tf_op jit(solution)/shard_map/convert_element_type | solution.py:149
  185.6 1.8 fusion.18
  187.5 0.8 copy-done.7
  188.3 1.5 fusion.1
  189.8 2.4 %copy.108 = bf16[1,512,1024]{2,1,0:T(8,128)(2,1)} copy(bf16[1,512,1024]{1,2,0:T(8,128)(2,1)} %bitcast.254) | data formatting | bytes 2097152
  192.2 3.9 %fusion.3 = bf16[1,512,8,128]{1,3,2,0:T(8,128)(2,1)} fusion(f32[8,128,512]{2,1,0:T(8,128)S(1)} %copy-done.8, bf16[512,8,128]{0,2,1:T(8,128)(2,1)S(1)} %bitcast.244, bf16[8,512,512]{2,1,0:T(8,128)(2,1)} %copy-done.1, f32[512,8]{0,1:T(8,128)S(1)} %get-tuple-element.40), kind=kOutput, calls=%fused_computation.8 | convolution fusion | flops 538443776 | bytes 8404992 | tf_op jit(solution)/shard_map/bhts,bthd->bshd/dot_general | solution.py:158
  196.1 2.3 %copy.107 = bf16[1,512,1024]{2,1,0:T(8,128)(2,1)} copy(bf16[1,512,1024]{1,2,0:T(8,128)(2,1)} %bitcast.255) | data formatting | bytes 2097152
  (77 shorter events, 0.2 us)
Async XLA Ops:
  7.2 42.6 %all-gather.14.cloned.1.call-start = ((), (), s32[]{:S(2)}) async-start(), calls=%async_computation.4 | async-start | bytes 2621440 | tf_op jit(solution)/shard_map/all_gather | solution.py:26
  8.7 57.3 %copy-start.2 = (bf16[64,8,8,128]{3,2,1,0:T(8,128)(2,1)}, bf16[64,8,8,128]{3,2,1,0:T(8,128)(2,1)S(1)}, u32[]{:S(2)}) copy-start(bf16[64,8,8,128]{3,2,1,0:T(8,128)(2,1)S(1)} %copy.117) | copy-start | bytes 3145732
  8.8 2.6 %copy-start.37 = (u32[256]{0:T(256)S(1)}, u32[256]{0:T(256)}, u32[]{:S(2)}) copy-start(u32[256]{0:T(256)} %constant.63) | copy-start | bytes 3076
  8.8 4.0 %copy-start.36 = (s32[8]{0:T(128)S(1)}, s32[8]{0:T(128)}, u32[]{:S(2)}) copy-start(s32[8]{0:T(128)} %param.19) | copy-start | bytes 100
  9.5 4.8 %copy-start.9 = (bf16[512,8,128]{0,2,1:T(8,128)(2,1)}, bf16[512,8,128]{0,2,1:T(8,128)(2,1)S(1)}, u32[]{:S(2)}) copy-start(bf16[512,8,128]{0,2,1:T(8,128)(2,1)S(1)} %copy.87) | copy-start | bytes 3145732
  11.3 57.8 %copy-start.4 = (bf16[64,8,8,128]{3,2,1,0:T(8,128)(2,1)}, bf16[64,8,8,128]{3,2,1,0:T(8,128)(2,1)S(1)}, u32[]{:S(2)}) copy-start(bf16[64,8,8,128]{3,2,1,0:T(8,128)(2,1)S(1)} %copy.118) | copy-start | bytes 3145732
  12.8 53.2 %copy-start.27 = (f32[8]{0:T(128)}, f32[8]{0:T(128)S(1)}, u32[]{:S(2)}) copy-start(f32[8]{0:T(128)S(1)} %get-tuple-element.26) | copy-start | bytes 100
  12.9 77.0 %copy-start.15 = (f32[512,8]{0,1:T(8,128)}, f32[512,8]{0,1:T(8,128)S(1)}, u32[]{:S(2)}) copy-start(f32[512,8]{0,1:T(8,128)S(1)} %get-tuple-element.42) | copy-start | bytes 49156
  14.3 72.7 %all-gather.10.cloned.1.call-start = ((), (), s32[]{:S(2)}) async-start(), calls=%async_computation.2 | async-start | bytes 2621440 | tf_op jit(solution)/shard_map/all_gather | solution.py:26
  24.4 119.7 %copy-start.20 = (f32[8]{0:T(128)}, f32[8]{0:T(128)S(1)}, u32[]{:S(2)}) copy-start(f32[8]{0:T(128)S(1)} %get-tuple-element.53) | copy-start | bytes 100
  24.4 119.7 %copy-start.24 = (f32[8]{0:T(128)}, f32[8]{0:T(128)S(1)}, u32[]{:S(2)}) copy-start(f32[8]{0:T(128)S(1)} %get-tuple-element.51) | copy-start | bytes 100
  25.1 119.0 %copy-start.18 = (f32[8]{0:T(128)}, f32[8]{0:T(128)S(1)}, u32[]{:S(2)}) copy-start(f32[8]{0:T(128)S(1)} %get-tuple-element.48) | copy-start | bytes 100
  25.1 119.0 %copy-start.22 = (f32[8]{0:T(128)}, f32[8]{0:T(128)S(1)}, u32[]{:S(2)}) copy-start(f32[8]{0:T(128)S(1)} %get-tuple-element.45) | copy-start | bytes 100
  52.3 13.7 %copy-start.34 = (f32[1,512]{1,0:T(1,128)S(1)}, f32[1,512]{1,0:T(1,128)}, u32[]{:S(2)}) copy-start(f32[1,512]{1,0:T(1,128)} %param.16) | copy-start | bytes 6148
  52.3 13.7 %copy-start.35 = (s32[1,512]{1,0:T(1,128)S(1)}, s32[1,512]{1,0:T(1,128)}, u32[]{:S(2)}) copy-start(s32[1,512]{1,0:T(1,128)} %param.15) | copy-start | bytes 6148
  52.4 91.7 %all-gather.16.cloned.1.call-start = ((), (), s32[]{:S(2)}) async-start(), calls=%async_computation.5 | async-start | bytes 2621440 | tf_op jit(solution)/shard_map/all_gather | solution.py:26
  65.8 3.4 %copy-start.13 = (pred[512,512]{1,0:T(8,128)(4,1)}, pred[512,512]{1,0:T(8,128)(4,1)S(1)}, u32[]{:S(2)}) copy-start(pred[512,512]{1,0:T(8,128)(4,1)S(1)} %fusion.13) | copy-start | bytes 786436
  66.0 3.2 %copy-start.11 = (f32[512,512]{1,0:T(8,128)}, f32[512,512]{1,0:T(8,128)S(1)}, u32[]{:S(2)}) copy-start(f32[512,512]{1,0:T(8,128)S(1)} %fusion.12) | copy-start | bytes 3145732
  69.2 2.0 copy-start
  86.9 3.0 %copy-start.6 = (f32[8,512,128]{1,2,0:T(8,128)S(1)}, f32[8,512,128]{1,2,0:T(8,128)}, u32[]{:S(2)}) copy-start(f32[8,512,128]{1,2,0:T(8,128)} %fusion.16) | copy-start | bytes 6291460
  91.9 1.9 copy-start.17
  116.6 30.1 %copy-start.33 = (f32[1,1,8]{2,1,0:T(1,128)S(1)}, f32[1,1,8]{2,1,0:T(1,128)}, u32[]{:S(2)}) copy-start(f32[1,1,8]{2,1,0:T(1,128)} %get-tuple-element.49) | copy-start | bytes 100
  116.6 66.0 %all-gather.12.cloned.1.call-start = ((), (), s32[]{:S(2)}) async-start(), calls=%async_computation.3 | async-start | bytes 2621440 | tf_op jit(solution)/shard_map/all_gather | solution.py:26
  157.6 18.3 %all-to-all-start.1 = ((f32[32,1,1024]{2,1,0:T(1,128)}), f32[32,1,1024]{2,1,0:T(1,128)S(1)}, u32[]{:S(2)}, u32[]{:S(2)}) async-start(f32[32,1,1024]{2,1,0:T(1,128)} %broadcast_in_dim.19), calls=%async_computation.1 | async-start | bytes 262144 | tf_op jit(solution)/shard_map/all_to_all | solution.py:38
  162.6 4.4 %copy-start.5 = (bf16[64,8,8,128]{3,2,1,0:T(8,128)(2,1)S(1)}, bf16[64,8,8,128]{3,2,1,0:T(8,128)(2,1)}, u32[]{:S(2)}) copy-start(bf16[64,8,8,128]{3,2,1,0:T(8,128)(2,1)} %copy-done.4) | copy-start | bytes 3145732
  162.7 4.4 %copy-start.12 = (f32[512,512]{1,0:T(8,128)S(1)}, f32[512,512]{1,0:T(8,128)}, u32[]{:S(2)}) copy-start(f32[512,512]{1,0:T(8,128)} %copy-done.11) | copy-start | bytes 3145732
  162.7 4.4 %copy-start.14 = (pred[512,512]{1,0:T(8,128)(4,1)S(1)}, pred[512,512]{1,0:T(8,128)(4,1)}, u32[]{:S(2)}) copy-start(pred[512,512]{1,0:T(8,128)(4,1)} %copy-done.13) | copy-start | bytes 786436
  162.7 4.4 %copy-start.28 = (f32[8]{0:T(128)S(1)}, f32[8]{0:T(128)}, u32[]{:S(2)}) copy-start(f32[8]{0:T(128)} %copy-done.27) | copy-start | bytes 100
  167.1 3.1 %copy-start.10 = (bf16[512,8,128]{0,2,1:T(8,128)(2,1)S(1)}, bf16[512,8,128]{0,2,1:T(8,128)(2,1)}, u32[]{:S(2)}) copy-start(bf16[512,8,128]{0,2,1:T(8,128)(2,1)} %copy-done.9) | copy-start | bytes 3145732
  170.2 2.0 copy-start.1
  170.2 2.0 copy-start.16
  173.6 9.0 %copy-start.19 = (f32[8]{0:T(128)S(1)}, f32[8]{0:T(128)}, u32[]{:S(2)}) copy-start(f32[8]{0:T(128)} %copy-done.18) | copy-start | bytes 100
  173.6 9.0 %copy-start.21 = (f32[8]{0:T(128)S(1)}, f32[8]{0:T(128)}, u32[]{:S(2)}) copy-start(f32[8]{0:T(128)} %copy-done.20) | copy-start | bytes 100
  173.6 9.0 %copy-start.23 = (f32[8]{0:T(128)S(1)}, f32[8]{0:T(128)}, u32[]{:S(2)}) copy-start(f32[8]{0:T(128)} %copy-done.22) | copy-start | bytes 100
  173.6 9.0 %copy-start.25 = (f32[8]{0:T(128)S(1)}, f32[8]{0:T(128)}, u32[]{:S(2)}) copy-start(f32[8]{0:T(128)} %copy-done.24) | copy-start | bytes 100
  173.6 9.0 %copy-start.26 = (f32[8]{0:T(128)S(1)}, f32[8]{0:T(128)}, u32[]{:S(2)}) copy-start(f32[8]{0:T(128)} %get-tuple-element.44) | copy-start | bytes 100
  173.7 9.0 %copy-start.29 = (f32[8]{0:T(128)S(1)}, f32[8]{0:T(128)}, u32[]{:S(2)}) copy-start(f32[8]{0:T(128)} %get-tuple-element.32) | copy-start | bytes 100
  173.7 9.0 %copy-start.30 = (f32[8]{0:T(128)S(1)}, f32[8]{0:T(128)}, u32[]{:S(2)}) copy-start(f32[8]{0:T(128)} %get-tuple-element.33) | copy-start | bytes 100
  173.7 9.0 %copy-start.31 = (f32[8]{0:T(128)S(1)}, f32[8]{0:T(128)}, u32[]{:S(2)}) copy-start(f32[8]{0:T(128)} %get-tuple-element.34) | copy-start | bytes 100
  173.7 9.0 %copy-start.32 = (f32[8]{0:T(128)S(1)}, f32[8]{0:T(128)}, u32[]{:S(2)}) copy-start(f32[8]{0:T(128)} %get-tuple-element.35) | copy-start | bytes 100
  185.6 1.9 copy-start.3
  185.6 2.7 %copy-start.7 = (f32[8,128,512]{2,1,0:T(8,128)S(1)}, f32[8,128,512]{2,1,0:T(8,128)}, u32[]{:S(2)}) copy-start(f32[8,128,512]{2,1,0:T(8,128)} %fusion.59) | copy-start | bytes 6291460
  189.8 2.4 %copy-start.8 = (f32[8,128,512]{2,1,0:T(8,128)S(1)}, f32[8,128,512]{2,1,0:T(8,128)}, u32[]{:S(2)}) copy-start(f32[8,128,512]{2,1,0:T(8,128)} %fusion.18) | copy-start | bytes 6291460
Sparse Core Ops, SparseCore 0:
  14.4 35.3 all-gather.13
  52.5 34.4 all-gather.9
  116.8 27.2 all-gather.15
  146.8 35.8 all-gather.11
where the time goes:
time: 206 us; the launch traced here: 205 us
  waiting for transfers between devices  71.1 us (35%)
  blocking collectives  44.1 us (21%)
  matrix products  28.1 us (14%)
  local copies, waits for them, and re-layouts  20.8 us (10%)
  other arithmetic  19.3 us (9%)
  between operations  16.3 us (8%)
  starting transfers between devices  5.17 us (3%)
    all_gather x4, waiting for transfers between devices, prefix_by_axis(): pieces = jax.tree.map(lambda part: lax.all_gather(part, axis), running)  71 us
    all_gather x2, blocking collectives, prefix_by_axis(): pieces = jax.tree.map(lambda part: lax.all_gather(part, axis), running)  19.3 us
    all_to_all x1, blocking collectives, sent_to_all(): lax.all_to_all(jnp.broadcast_to(value[None], (count, *value.shape)), axis...  14.8 us
    unnamed x83, local copies, waits for them, and re-layouts  14.4 us
    unnamed x1, blocking collectives  9.99 us
    add x2, other arithmetic, combine_states(): later[1] + later[0][None, :, None, None] * earlier[1]  5.11 us
    all_to_all x1, starting transfers between devices, sent_to_all(): lax.all_to_all(jnp.broadcast_to(value[None], (count, *value.shape)), axis...  5 us
    dot_general x1, matrix products, on_device(): jnp.einsum('bhts,bthe->bshe', score_half, grad_heads, preferred_element_t...  4.39 us
  transfers between devices with their start and end apart: 5, of which 4 were waited for; matrix products, arithmetic and copies ran while one was open for 12% of the time, Pallas kernels for 0%

commit v1 on v0

v1 whole, which is shorter than its diff:
```python
import functools

import jax
import jax.numpy as jnp
from jax import lax
from jax.experimental import pallas as pl
from jax.experimental.pallas import tpu as pltpu
from jax.sharding import PartitionSpec as P

clip_high = 1.28
epsilon = 1e-06
F32 = jnp.float32
BF16 = jnp.bfloat16
LANES = 128
HALF = 256


def dot_nn(a, b):
    return lax.dot_general(a, b, (((1,), (0,)), ((), ())), preferred_element_type=F32)


def dot_nt(a, b):
    return lax.dot_general(a, b, (((1,), (1,)), ((), ())), preferred_element_type=F32)


def dot_tn(a, b):
    return lax.dot_general(a, b, (((0,), (0,)), ((), ())), preferred_element_type=F32)


def rate_of(index, slab):
    return (16.0 / slab) * jnp.exp2(jnp.full((1, LANES), -index.astype(F32), F32))


def row_powers(rate, first, step, rows):
    at = lax.broadcasted_iota(jnp.int32, (rows, LANES), 0).astype(F32)
    return jnp.exp2(-rate * (first + step * at))


def decay_blocks(rate, transposed):
    rate2 = jnp.concatenate([rate] * (HALF // LANES), axis=1)
    rows = lax.broadcasted_iota(jnp.int32, (HALF, HALF), 0)
    cols = lax.broadcasted_iota(jnp.int32, (HALF, HALF), 1)
    lag = (cols - rows if transposed else rows - cols).astype(F32)
    diagonal = jnp.where(lag >= 0, jnp.exp2(-rate2 * jnp.maximum(lag, 0.0)), 0.0)
    below = jnp.exp2(-rate2 * (lag + float(HALF)))
    return diagonal, below


def to_columns(row):
    parts = []
    for at in range(0, row.shape[1], LANES):
        parts.append(jnp.broadcast_to(row[:, at : at + LANES], (LANES, LANES)).T)
    return jnp.concatenate(parts, axis=0)


def head(ref, i):
    return ref[0, :, i * LANES : (i + 1) * LANES]


def state_kernel(per_step, slab, index_ref, k_ref, v_ref, out_ref):
    for i in range(per_step):
        rate = rate_of(index_ref[pl.program_id(0) * per_step + i], slab)
        decayed = head(k_ref, i).astype(F32) * row_powers(rate, slab - 1.0, -1.0, slab)
        out_ref[i] = dot_tn(decayed.astype(BF16), head(v_ref, i))


def scan_kernel(slabs, slab, reverse, index_ref, x_ref, out_ref):
    rate = rate_of(index_ref[0], slab)
    factor = jnp.exp2(-rate * float(slab))
    running = jnp.zeros(x_ref.shape[1:], F32)
    for j in reversed(range(slabs)) if reverse else range(slabs):
        out_ref[j] = running
        running = factor * running + x_ref[j]


def scan_gain_kernel(slabs, slab, index_ref, x_ref, g_ref, out_ref):
    rate = rate_of(index_ref[0], slab)
    factor = jnp.exp2(-rate * float(slab))
    rows = x_ref.shape[1]
    running = jnp.zeros(x_ref.shape[1:], F32)
    for j in reversed(range(slabs)):
        out_ref[j, :rows] = running
        out_ref[j, rows:] = g_ref[...]
        running = factor * running + x_ref[j]


def local_kernel(
    per_step, slab, total, index_ref, place_ref, length_ref, advantage_ref, q_ref, k_ref, v_ref, mask_ref, imp_ref,
    out_ref, weight_ref,
):
    @pl.when(pl.program_id(0) == 0)
    def _():
        at = place_ref[0] * slab + lax.broadcasted_iota(jnp.int32, (1, slab), 1)
        inside = (at < length_ref[0]).astype(F32)
        length = jnp.full((1, slab), length_ref[0].astype(F32), F32)
        weight = mask_ref[...].astype(F32) * inside * jnp.minimum(imp_ref[...], clip_high)
        weight = weight * advantage_ref[0] * (float(total) / length)
        weight_ref[...] = to_columns(weight)

    for i in range(per_step):
        rate = rate_of(index_ref[pl.program_id(0) * per_step + i], slab)
        diagonal, below = decay_blocks(rate, False)
        q, k, v = head(q_ref, i), head(k_ref, i), head(v_ref, i)
        lanes = slice(i * LANES, (i + 1) * LANES)
        for r in range(slab // HALF):
            scores = dot_nt(q[r * HALF : (r + 1) * HALF], k[: (r + 1) * HALF])
            table = diagonal if r == 0 else jnp.concatenate([below, diagonal], axis=1)
            probs = (scores * table).astype(BF16)
            out_ref[r * HALF : (r + 1) * HALF, lanes] = dot_nn(probs, v[: (r + 1) * HALF])


def output_kernel(
    per_step, slab, index_ref, q_ref, s_ref, local_ref, c_ref, weight_ref, gain_ref, out_ref, stat_ref, square, cross
):
    step = pl.program_id(0)
    squares = jnp.zeros((slab, LANES), F32)
    crosses = jnp.zeros((slab, LANES), F32)
    for i in range(per_step):
        rate = rate_of(index_ref[step * per_step + i], slab)
        lanes = slice(i * LANES, (i + 1) * LANES)
        carried = dot_nn(head(q_ref, i), s_ref[i].astype(BF16))
        out = local_ref[:, lanes] + carried * row_powers(rate, 1.0, 1.0, slab)
        out_ref[:, lanes] = out
        grad_n = head(c_ref, i).astype(F32) * weight_ref[...] * gain_ref[:, lanes]
        squares += out * out
        crosses += grad_n * out

    @pl.when(step == 0)
    def _():
        square[...] = squares
        cross[...] = crosses

    @pl.when(step != 0)
    def _():
        square[...] += squares
        cross[...] += crosses

    @pl.when(step == pl.num_programs(0) - 1)
    def _():
        rows = []
        for ref in (square, cross):
            for at in range(0, slab, LANES):
                rows.append(jnp.sum(ref[at : at + LANES, :].T, axis=0, keepdims=True))
        stats = jnp.concatenate(rows, axis=0)
        for d in range(stat_ref.shape[0]):
            stat_ref[d] = stats


def grad_kernel(
    per_step, slab, features, index_ref, stat_ref, q_ref, o_ref, c_ref, weight_ref, gain_ref,
    g_ref, ret_ref, gain_out_ref, inv_ref, mean_ref, inv_col, mean_col,
):
    step = pl.program_id(0)

    @pl.when(step == 0)
    def _():
        stats = jnp.sum(stat_ref[...], axis=0)
        blocks = slab // LANES
        inverse = lax.rsqrt(stats[:blocks] / features + epsilon)
        mean = stats[blocks : 2 * blocks] * inverse / features
        for b in range(blocks):
            rows = slice(b * LANES, (b + 1) * LANES)
            inv_col[rows, :] = jnp.broadcast_to(inverse[b : b + 1], (LANES, LANES)).T
            mean_col[rows, :] = jnp.broadcast_to(mean[b : b + 1], (LANES, LANES)).T
        inv_ref[...] = inv_col[...]
        mean_ref[...] = mean_col[...]

    for i in range(per_step):
        rate = rate_of(index_ref[step * per_step + i], slab)
        lanes = slice(i * LANES, (i + 1) * LANES)
        inverse = inv_col[...]
        normed = o_ref[:, lanes] * inverse
        grad_y = head(c_ref, i).astype(F32) * weight_ref[...]
        grad_n = grad_y * gain_ref[:, lanes]
        grad_out = (inverse * (grad_n - normed * mean_col[...])).astype(BF16)
        g_ref[:, lanes] = grad_out
        gain_out_ref[pl.ds(step * per_step + i, 1), :] = jnp.sum(grad_y * normed, axis=0, keepdims=True)
        decayed = head(q_ref, i).astype(F32) * row_powers(rate, 0.0, 1.0, slab)
        ret_ref[i] = dot_tn(decayed.astype(BF16), grad_out)


def backward_kernel(
    per_step, slab, index_ref, q_ref, k_ref, v_ref, g_ref, s_ref, o_ref, inv_ref, gain_ref,
    mixed_ref, qg_ref, kl_ref, vl_ref,
):
    for i in range(per_step):
        rate = rate_of(index_ref[pl.program_id(0) * per_step + i], slab)
        lanes = slice(i * LANES, (i + 1) * LANES)
        mixed_ref[0, :, lanes] = (o_ref[:, lanes] * inv_ref[...] * gain_ref[:, lanes]).astype(BF16)
        q, k, v, g = head(q_ref, i), head(k_ref, i), head(v_ref, i), g_ref[:, lanes]
        diagonal, below = decay_blocks(rate, False)
        diagonal_t, below_t = decay_blocks(rate, True)
        carried = dot_nt(g, s_ref[i].astype(BF16)) * row_powers(rate, 1.0, 1.0, slab)
        a, b = slice(0, HALF), slice(HALF, 2 * HALF)
        upper = (dot_nt(g[a], v[a]) * diagonal).astype(BF16)
        lower = (dot_nt(g[b], v) * jnp.concatenate([below, diagonal], axis=1)).astype(BF16)
        qg_ref[0, a, lanes] = (dot_nn(upper, k[a]) + carried[a]).astype(BF16)
        qg_ref[0, b, lanes] = (dot_nn(lower, k) + carried[b]).astype(BF16)
        table = jnp.concatenate([diagonal_t, below_t], axis=1)
        for x, y, z, ref in ((v, g, q, kl_ref), (k, q, g, vl_ref)):
            first = (dot_nt(x[a], y) * table).astype(BF16)
            second = (dot_nt(x[b], y[b]) * diagonal_t).astype(BF16)
            ref[a, lanes] = dot_nn(first, z)
            ref[b, lanes] = dot_nn(second, z[b])


def final_kernel(per_step, slab, rows, index_ref, r_ref, k_ref, v_ref, kl_ref, vl_ref, kg_ref, vg_ref, gain_ref):
    step = pl.program_id(0)
    pieces = LANES // rows
    gains = jnp.zeros(gain_ref.shape, F32)
    for i in range(per_step):
        rate = rate_of(index_ref[step * per_step + i], slab)
        lanes = slice(i * LANES, (i + 1) * LANES)
        to_next = row_powers(rate, float(slab), -1.0, slab)
        back = jnp.concatenate([r_ref[i * pieces + p, :rows] for p in range(pieces)], axis=0).astype(BF16)
        kg_ref[0, :, lanes] = (kl_ref[:, lanes] + dot_nt(head(v_ref, i), back) * to_next).astype(BF16)
        vg_ref[0, :, lanes] = (vl_ref[:, lanes] + dot_nn(head(k_ref, i), back) * to_next).astype(BF16)
        for p in range(pieces):
            gains += r_ref[i * pieces + p, rows:]

    @pl.when(step == 0)
    def _():
        gain_ref[...] = gains

    @pl.when(step != 0)
    def _():
        gain_ref[...] += gains


def on_device(query_rows, key_rows, value_rows, norm_gain, cotangent, loss_mask, importance, advantage, lengths, decay_index):
    _, slab, features = query_rows.shape
    heads = decay_index.shape[0]
    slabs = lax.axis_size("seq")
    place = lax.axis_index("seq")
    rows = heads * LANES // slabs
    total_features = float(features * lax.axis_size("head"))
    per_step = 2
    steps = heads // per_step
    wide = per_step * LANES
    gain_row = norm_gain.reshape(1, features)

    smem = pl.BlockSpec(memory_space=pltpu.SMEM)
    token = pl.BlockSpec((1, slab, wide), lambda i: (0, 0, i))
    flat = pl.BlockSpec((slab, wide), lambda i: (0, i))
    column = pl.BlockSpec((slab, LANES), lambda i: (0, 0))
    gain_spec = pl.BlockSpec((1, wide), lambda i: (0, i))
    state = pl.BlockSpec((per_step, LANES, LANES), lambda i: (i, 0, 0))
    token_f32 = jax.ShapeDtypeStruct((slab, features), F32)
    column_f32 = jax.ShapeDtypeStruct((slab, LANES), F32)
    token_out = jax.ShapeDtypeStruct(query_rows.shape, BF16)
    state_f32 = jax.ShapeDtypeStruct((heads, LANES, LANES), F32)
    params = pltpu.CompilerParams(dimension_semantics=("arbitrary",))

    def over_slabs(pieces):
        return lax.all_to_all(pieces, "seq", 0, 0, tiled=True)

    own_head = lax.dynamic_slice(decay_index, (place * rows // LANES,), (1,))

    state_local = pl.pallas_call(
        functools.partial(state_kernel, per_step, slab),
        grid=(steps,),
        in_specs=[smem, token, token],
        out_specs=state,
        out_shape=state_f32,
        compiler_params=params,
        name="state_local",
    )(decay_index, key_rows, value_rows)
    sent = over_slabs(state_local.reshape(slabs, rows, LANES))

    local_out, weight = pl.pallas_call(
        functools.partial(local_kernel, per_step, slab, slab * slabs),
        grid=(steps,),
        in_specs=[smem, smem, smem, smem, token, token, token]
        + [pl.BlockSpec((1, slab), lambda i: (0, 0))] * 2,
        out_specs=[flat, column],
        out_shape=[token_f32, column_f32],
        compiler_params=params,
        name="local_attention",
    )(decay_index, place.reshape(1), lengths, advantage, query_rows, key_rows, value_rows, loss_mask, importance)

    piece_f32 = jax.ShapeDtypeStruct((slabs, rows, LANES), F32)
    before = pl.pallas_call(
        functools.partial(scan_kernel, slabs, slab, False),
        in_specs=[smem, pl.BlockSpec(memory_space=pltpu.VMEM)],
        out_specs=pl.BlockSpec(memory_space=pltpu.VMEM),
        out_shape=piece_f32,
        name="prefix",
    )(own_head, sent)
    state_in = over_slabs(before).reshape(heads, LANES, LANES)

    groups = lax.axis_size("head")
    stat_rows = 2 * slab // LANES
    outputs, stats = pl.pallas_call(
        functools.partial(output_kernel, per_step, slab),
        grid=(steps,),
        in_specs=[smem, token, state, flat, token, column, gain_spec],
        out_specs=[flat, pl.BlockSpec((groups, stat_rows, LANES), lambda i: (0, 0, 0))],
        out_shape=[token_f32, jax.ShapeDtypeStruct((groups, stat_rows, LANES), F32)],
        scratch_shapes=[pltpu.VMEM((slab, LANES), F32)] * 2,
        compiler_params=params,
        name="outputs",
    )(decay_index, query_rows, state_in, local_out, cotangent, weight, gain_row)
    stats = lax.all_to_all(stats, "head", 0, 0, tiled=True)

    grad_out, return_local, gain_part, inverse, _ = pl.pallas_call(
        functools.partial(grad_kernel, per_step, slab, total_features),
        grid=(steps,),
        in_specs=[
            smem, pl.BlockSpec((groups, stat_rows, LANES), lambda i: (0, 0, 0)), token, flat, token, column, gain_spec
        ],
        out_specs=[flat, state, pl.BlockSpec((heads, LANES), lambda i: (0, 0)), column, column],
        out_shape=[
            jax.ShapeDtypeStruct((slab, features), BF16), state_f32, jax.ShapeDtypeStruct((heads, LANES), F32),
            column_f32, column_f32,
        ],
        scratch_shapes=[pltpu.VMEM((slab, LANES), F32)] * 2,
        compiler_params=params,
        name="output_grad",
    )(decay_index, stats, query_rows, outputs, cotangent, weight, gain_row)
    returned = over_slabs(return_local.reshape(slabs, rows, LANES))
    gain_part = lax.psum(gain_part, "dp")

    mixed, query_grad, key_local, value_local = pl.pallas_call(
        functools.partial(backward_kernel, per_step, slab),
        grid=(steps,),
        in_specs=[smem, token, token, token, flat, state, flat, column, gain_spec],
        out_specs=[token, token, flat, flat],
        out_shape=[token_out, token_out, token_f32, token_f32],
        compiler_params=params,
        name="local_grads",
    )(decay_index, query_rows, key_rows, value_rows, grad_out, state_in, outputs, inverse, gain_row)

    after = pl.pallas_call(
        functools.partial(scan_gain_kernel, slabs, slab),
        in_specs=[smem, pl.BlockSpec(memory_space=pltpu.VMEM), pl.BlockSpec(memory_space=pltpu.VMEM)],
        out_specs=pl.BlockSpec(memory_space=pltpu.VMEM),
        out_shape=jax.ShapeDtypeStruct((slabs, rows + heads, LANES), F32),
        name="suffix",
    )(own_head, returned, gain_part)
    return_in = over_slabs(after)

    pieces = LANES // rows
    key_grad, value_grad, gain_grad = pl.pallas_call(
        functools.partial(final_kernel, per_step, slab, rows),
        grid=(steps,),
        in_specs=[
            smem, pl.BlockSpec((per_step * pieces, rows + heads, LANES), lambda i: (i, 0, 0)), token, token, flat, flat
        ],
        out_specs=[token, token, pl.BlockSpec((heads, LANES), lambda i: (0, 0))],
        out_shape=[token_out, token_out, jax.ShapeDtypeStruct((heads, LANES), F32)],
        compiler_params=params,
        name="final_grads",
    )(decay_index, return_in, key_rows, value_rows, key_local, value_local)
    return (mixed, query_grad, key_grad, value_grad, gain_grad.reshape(features))


def solution(mesh):
    tokens = P("dp", "seq", "head")
    return jax.shard_map(
        on_device,
        mesh=mesh,
        in_specs=(
            tokens, tokens, tokens, P("head"), tokens, P("dp", "seq"), P("dp", "seq"), P("dp"), P("dp"), P("head"),
        ),
        out_specs=(tokens, tokens, tokens, tokens, P("head")),
        check_vma=False,
    )
```

time: 206 us -> 107 us (0.52)
  waiting for transfers between devices: 71.1 us -> 16.8 us
  Pallas kernels: 0 us -> 41.1 us
  matrix products: 28.1 us -> 0 us
  blocking collectives: 44.1 us -> 19.8 us
  other arithmetic: 19.3 us -> 0 us
  starting transfers between devices: 5.17 us -> 22.8 us
  local copies, waits for them, and re-layouts: 20.8 us -> 3.8 us
  between operations: 16.3 us -> 1.97 us
    all_gather x4 -> x0, waiting for transfers between devices: 71 us -> none  [prefix_by_axis(): pieces = jax.tree.map(lambda part: lax.all_gather(part, axis), running)]
    pallas_call x0 -> x8, Pallas kernels: none -> 41.1 us  [the longest x1 9.67 us: on_device(): pl.pallas_call(functools.partial(backward_kernel, per_step, slab), grid=(...]
    dot_general x12 -> x0, matrix products: 28.1 us -> none  [the longest x1 4.39 us: on_device(): jnp.einsum('bhts,bthe->bshe', score_half, grad_heads, preferred_element_t...]
    all_gather x2 -> x0, blocking collectives: 19.3 us -> none  [prefix_by_axis(): pieces = jax.tree.map(lambda part: lax.all_gather(part, axis), running)]
    all_to_all x1 -> x4, starting transfers between devices: 5 us -> 22.8 us  [over_slabs(): return lax.all_to_all(pieces, 'seq', 0, 0, tiled=True)]
    all_to_all x1 -> x4, waiting for transfers between devices: 0.01 us -> 16.8 us  [over_slabs(): return lax.all_to_all(pieces, 'seq', 0, 0, tiled=True)]
    unnamed x83 -> x10, local copies, waits for them, and re-layouts: 14.4 us -> 3.21 us
    unnamed x1 -> x0, blocking collectives: 9.99 us -> none
  transfers between devices with their start and end apart: 5 -> 4, of which waited for: 4 -> 3; matrix products, arithmetic and copies ran while one was open for 12% -> 1% of each run, Pallas kernels for 0% -> 15%
where the time goes in v1:
time: 107 us; the launch traced here: 106 us
  Pallas kernels  41.1 us (38%)
  starting transfers between devices  22.8 us (21%)
  blocking collectives  19.8 us (19%)
  waiting for transfers between devices  16.8 us (16%)
  local copies, waits for them, and re-layouts  3.8 us (4%)
  between operations  1.97 us (2%)
    all_to_all x4, starting transfers between devices, over_slabs(): return lax.all_to_all(pieces, 'seq', 0, 0, tiled=True)  22.8 us
    all_to_all x4, waiting for transfers between devices, over_slabs(): return lax.all_to_all(pieces, 'seq', 0, 0, tiled=True)  16.8 us
    all_to_all x1, blocking collectives, on_device(): stats = lax.all_to_all(stats, 'head', 0, 0, tiled=True)  16.6 us
    pallas_call x1, Pallas kernels, on_device(): pl.pallas_call(functools.partial(backward_kernel, per_step, slab), grid=(...  9.67 us
    pallas_call x1, Pallas kernels, on_device(): pl.pallas_call(functools.partial(local_kernel, per_step, slab, slab * sla...  6.37 us
    pallas_call x1, Pallas kernels, on_device(): pl.pallas_call(functools.partial(output_kernel, per_step, slab), grid=(st...  5.52 us
    pallas_call x1, Pallas kernels, on_device(): pl.pallas_call(functools.partial(final_kernel, per_step, slab, rows), gri...  5.24 us
    pallas_call x1, Pallas kernels, on_device(): pl.pallas_call(functools.partial(grad_kernel, per_step, slab, total_featu...  5.23 us
  transfers between devices with their start and end apart: 4, of which 3 were waited for; matrix products, arithmetic and copies ran while one was open for 1% of the time, Pallas kernels for 15%

profile of v1, /device:TPU:2, one launch (start us, length us, event | category | flops | bytes accessed | tf_op | source)
XLA Modules:
  0.0 106.2 jit_solution(18119119777162476647)
XLA Ops:
  0.6 0.0 copy-start.4
  0.6 4.1 %state_local.1 = f32[8,128,128]{2,1,0:T(8,128)} custom-call(s32[8]{0:T(128)} %index_ref.11, bf16[1,512,1024]{2,1,0:T(8,128)(2,1)} %k_ref.7, bf16[1,512,1024]{2,1,0:T(8,128)(2,1)} %v_ref.7), custom_call_target="tpu_custom_call" | custom-call | tf_op jit(solution)/shard_map/state_local/pallas_call | solution.py:259
  4.8 7.5 %all-to-all-start = ((f32[16,64,128]{2,1,0:T(8,128)}), f32[16,64,128]{2,1,0:T(8,128)S(1)}, u32[]{:S(2)}, u32[]{:S(2)}) async-start(f32[16,64,128]{2,1,0:T(8,128)} %bitcast.8), calls=%async_computation | async-start | bytes 1048576 | tf_op jit(solution)/shard_map/all_to_all | solution.py:255
  12.2 0.0 copy-done.4
  12.2 0.6 dynamic_slice.3.index_ref
  12.8 9.6 %all-to-all-done.x_ref = f32[16,64,128]{2,1,0:T(8,128)S(1)} async-done(((f32[16,64,128]{2,1,0:T(8,128)}), f32[16,64,128]{2,1,0:T(8,128)S(1)}, u32[]{:S(2)}, u32[]{:S(2)}) %all-to-all-start) | async-done | bytes 524320 | tf_op jit(solution)/shard_map/all_to_all | solution.py:255
  22.4 0.0 copy-start.2
  22.4 0.8 copy-done.2
  23.2 2.5 %prefix.1 = f32[16,64,128]{2,1,0:T(8,128)} custom-call(s32[1]{0:T(128)} %dynamic_slice.3.index_ref, f32[16,64,128]{2,1,0:T(8,128)} %copy-done.2), custom_call_target="tpu_custom_call" | custom-call | tf_op jit(solution)/shard_map/prefix/pallas_call | solution.py:282
  25.7 4.8 %all-to-all-start.1 = ((f32[16,64,128]{2,1,0:T(8,128)}), f32[16,64,128]{2,1,0:T(8,128)S(1)}, u32[]{:S(2)}, u32[]{:S(2)}) async-start(f32[16,64,128]{2,1,0:T(8,128)} %prefix.1), calls=%async_computation.1 | async-start | bytes 1048576 | tf_op jit(solution)/shard_map/all_to_all | solution.py:255
  31.8 6.4 %local_attention.1 = (f32[512,1024]{1,0:T(8,128)}, f32[512,128]{1,0:T(8,128)}) custom-call(s32[8]{0:T(128)} %index_ref.11, s32[1]{0:T(128)} %bitcast.2.place_ref, s32[1]{0:T(128)S(6)} %copy.16.length_ref, f32[1]{0:T(128)S(6)} %copy.15.advantage_ref, bf16[1,512,1024]{2,1,0:T(8,128)(2,1)} %q_ref.7, bf16[1,512,1024]{2,1,0:T(8,128)(2,1)} %k_ref.7, ...), custom_call_target="tpu_custom_call" | custom-call | tf_op jit(solution)/shard_map/local_attention/pallas_call | solution.py:270
  38.1 1.6 %all-to-all-done.1 = f32[16,64,128]{2,1,0:T(8,128)S(1)} async-done(((f32[16,64,128]{2,1,0:T(8,128)}), f32[16,64,128]{2,1,0:T(8,128)S(1)}, u32[]{:S(2)}, u32[]{:S(2)}) %all-to-all-start.1) | async-done | bytes 524320 | tf_op jit(solution)/shard_map/all_to_all | solution.py:255
  39.8 0.0 copy-start
  39.8 0.8 copy-done
  40.6 5.5 %outputs.1 = (f32[512,1024]{1,0:T(8,128)}, f32[8,8,128]{2,1,0:T(8,128)}) custom-call(s32[8]{0:T(128)} %index_ref.11, bf16[1,512,1024]{2,1,0:T(8,128)(2,1)} %q_ref.7, f32[8,128,128]{2,1,0:T(8,128)} %bitcast.6, f32[512,1024]{1,0:T(8,128)} %get-tuple-element.20.local_ref, bf16[1,512,1024]{2,1,0:T(8,128)(2,1)} %c_ref.3, ...), custom_call_target="tpu_custom_call" | custom-call | tf_op jit(solution)/shard_map/outputs/pallas_call | solution.py:293
  46.1 16.6 %all_to_all.25.stat_ref = f32[8,8,128]{2,1,0:T(8,128)} all-to-all(f32[8,8,128]{2,1,0:T(8,128)} %get-tuple-element.22), channel_id=1, replica_groups=mesh['dp'=2,'seq'=16,'head'=8] {'head'}, dimensions={0} | all-to-all | bytes 65536 | tf_op jit(solution)/shard_map/all_to_all | solution.py:303
  62.7 5.2 %output_grad.1 = (bf16[512,1024]{1,0:T(8,128)(2,1)}, f32[8,128,128]{2,1,0:T(8,128)}, f32[8,128]{1,0:T(8,128)}, f32[512,128]{1,0:T(8,128)}, f32[512,128]{1,0:T(8,128)}) custom-call(s32[8]{0:T(128)} %index_ref.11, f32[8,8,128]{2,1,0:T(8,128)} %all_to_all.25.stat_ref, bf16[1,512,1024]{2,1,0:T(8,128)(2,1)} %q_ref.7, f32[512,1024]{1,0:T(8,128)} %get-tuple-element.23.o_ref, ...), custom_call_target="tpu_custom_call" | custom-call | tf_op jit(solution)/shard_map/output_grad/pallas_call | solution.py:305
  67.9 5.7 %all-to-all-start.3 = ((f32[16,64,128]{2,1,0:T(8,128)}), f32[16,64,128]{2,1,0:T(8,128)S(1)}, u32[]{:S(2)}, u32[]{:S(2)}) async-start(f32[16,64,128]{2,1,0:T(8,128)} %bitcast.9), calls=%async_computation.3 | async-start | bytes 1048576 | tf_op jit(solution)/shard_map/all_to_all | solution.py:255
  73.6 3.2 %psum.7.g_ref = f32[8,128]{1,0:T(8,128)} all-reduce(f32[8,128]{1,0:T(8,128)} %get-tuple-element.29), channel_id=1, replica_groups=mesh['dp'=2,'seq'=16,'head'=8] {'dp'}, use_global_device_ids=true, to_apply=%region_0.1 | all-reduce | flops 1024 | bytes 8192 | tf_op jit(solution)/shard_map/psum | solution.py:321
  76.8 5.6 %all-to-all-done.3.x_ref = f32[16,64,128]{2,1,0:T(8,128)S(1)} async-done(((f32[16,64,128]{2,1,0:T(8,128)}), f32[16,64,128]{2,1,0:T(8,128)S(1)}, u32[]{:S(2)}, u32[]{:S(2)}) %all-to-all-start.3) | async-done | bytes 524320 | tf_op jit(solution)/shard_map/all_to_all | solution.py:255
  82.4 0.0 copy-start.3
  82.4 0.8 copy-done.3
  83.2 2.5 %suffix.1 = f32[16,72,128]{2,1,0:T(8,128)} custom-call(s32[1]{0:T(128)} %dynamic_slice.3.index_ref, f32[16,64,128]{2,1,0:T(8,128)} %copy-done.3, f32[8,128]{1,0:T(8,128)} %psum.7.g_ref), custom_call_target="tpu_custom_call" | custom-call | tf_op jit(solution)/shard_map/suffix/pallas_call | solution.py:333
  85.7 4.8 %all-to-all-start.4 = ((f32[16,72,128]{2,1,0:T(8,128)}), f32[16,72,128]{2,1,0:T(8,128)S(1)}, u32[]{:S(2)}, u32[]{:S(2)}) async-start(f32[16,72,128]{2,1,0:T(8,128)} %suffix.1), calls=%async_computation.4 | async-start | bytes 1179648 | tf_op jit(solution)/shard_map/all_to_all | solution.py:255
  90.5 9.7 %local_grads.1 = (bf16[1,512,1024]{2,1,0:T(8,128)(2,1)}, bf16[1,512,1024]{2,1,0:T(8,128)(2,1)}, f32[512,1024]{1,0:T(8,128)}, f32[512,1024]{1,0:T(8,128)}) custom-call(s32[8]{0:T(128)} %index_ref.11, bf16[1,512,1024]{2,1,0:T(8,128)(2,1)} %q_ref.7, bf16[1,512,1024]{2,1,0:T(8,128)(2,1)} %k_ref.7, bf16[1,512,1024]{2,1,0:T(8,128)(2,1)} %v_ref.7, ...), custom_call_target="tpu_custom_call" | custom-call | tf_op jit(solution)/shard_map/local_grads/pallas_call | solution.py:323
  100.2 0.0 all-to-all-done.4.r_ref
  100.2 0.0 copy-start.1
  100.2 0.8 copy-done.1
  101.0 5.2 %final_grads.1 = (bf16[1,512,1024]{2,1,0:T(8,128)(2,1)}, bf16[1,512,1024]{2,1,0:T(8,128)(2,1)}, f32[8,128]{1,0:T(8,128)}) custom-call(s32[8]{0:T(128)} %index_ref.11, f32[16,72,128]{2,1,0:T(8,128)} %copy-done.1, bf16[1,512,1024]{2,1,0:T(8,128)(2,1)} %k_ref.7, bf16[1,512,1024]{2,1,0:T(8,128)(2,1)} %v_ref.7, f32[512,1024]{1,0:T(8,128)} %get-tuple-element.30.kl_ref, ...), custom_call_target="tpu_custom_call" | custom-call | tf_op jit(solution)/shard_map/final_grads/pallas_call | solution.py:343
Async XLA Ops:
  0.6 11.6 %copy-start.4 = (s32[8]{0:T(128)S(1)}, s32[8]{0:T(128)}, u32[]{:S(2)}) copy-start(s32[8]{0:T(128)} %index_ref.11) | copy-start | bytes 100
  4.8 17.7 %all-to-all-start = ((f32[16,64,128]{2,1,0:T(8,128)}), f32[16,64,128]{2,1,0:T(8,128)S(1)}, u32[]{:S(2)}, u32[]{:S(2)}) async-start(f32[16,64,128]{2,1,0:T(8,128)} %bitcast.8), calls=%async_computation | async-start | bytes 1048576 | tf_op jit(solution)/shard_map/all_to_all | solution.py:255
  22.4 0.8 copy-start.2
  25.7 14.1 %all-to-all-start.1 = ((f32[16,64,128]{2,1,0:T(8,128)}), f32[16,64,128]{2,1,0:T(8,128)S(1)}, u32[]{:S(2)}, u32[]{:S(2)}) async-start(f32[16,64,128]{2,1,0:T(8,128)} %prefix.1), calls=%async_computation.1 | async-start | bytes 1048576 | tf_op jit(solution)/shard_map/all_to_all | solution.py:255
  39.8 0.8 copy-start
  67.9 14.5 %all-to-all-start.3 = ((f32[16,64,128]{2,1,0:T(8,128)}), f32[16,64,128]{2,1,0:T(8,128)S(1)}, u32[]{:S(2)}, u32[]{:S(2)}) async-start(f32[16,64,128]{2,1,0:T(8,128)} %bitcast.9), calls=%async_computation.3 | async-start | bytes 1048576 | tf_op jit(solution)/shard_map/all_to_all | solution.py:255
  82.4 0.8 copy-start.3
  85.7 14.5 %all-to-all-start.4 = ((f32[16,72,128]{2,1,0:T(8,128)}), f32[16,72,128]{2,1,0:T(8,128)S(1)}, u32[]{:S(2)}, u32[]{:S(2)}) async-start(f32[16,72,128]{2,1,0:T(8,128)} %suffix.1), calls=%async_computation.4 | async-start | bytes 1179648 | tf_op jit(solution)/shard_map/all_to_all | solution.py:255
  100.2 0.8 copy-start.1

commit v2 on v1

v2 whole, which is shorter than its diff:
```python
import functools

import jax
import jax.numpy as jnp
from jax import lax
from jax.experimental import pallas as pl
from jax.experimental.pallas import tpu as pltpu
from jax.sharding import PartitionSpec as P

clip_high = 1.28
epsilon = 1e-06
F32 = jnp.float32
BF16 = jnp.bfloat16
LANES = 128
HALF = 256


def dot_nn(a, b):
    return lax.dot_general(a, b, (((1,), (0,)), ((), ())), preferred_element_type=F32)


def dot_nt(a, b):
    return lax.dot_general(a, b, (((1,), (1,)), ((), ())), preferred_element_type=F32)


def dot_tn(a, b):
    return lax.dot_general(a, b, (((0,), (0,)), ((), ())), preferred_element_type=F32)


def rate_of(index, slab):
    return (16.0 / slab) * jnp.exp2(jnp.full((1, LANES), -index.astype(F32), F32))


def row_powers(rate, first, step, rows):
    at = lax.broadcasted_iota(jnp.int32, (LANES, LANES), 0).astype(F32)
    powers = jnp.exp2(-rate * (first + step * at))
    parts = [powers] + [powers * jnp.exp2(-rate * (step * b)) for b in range(LANES, rows, LANES)]
    return jnp.concatenate(parts, axis=0) if len(parts) > 1 else powers


def decay_blocks(rate, transposed):
    rate2 = jnp.concatenate([rate] * (HALF // LANES), axis=1)
    rows = lax.broadcasted_iota(jnp.int32, (HALF, HALF), 0)
    cols = lax.broadcasted_iota(jnp.int32, (HALF, HALF), 1)
    lag = (cols - rows if transposed else rows - cols).astype(F32)
    powers = jnp.exp2(-rate2 * lag)
    return jnp.where(lag >= 0, powers, 0.0), powers * jnp.exp2(-rate2 * float(HALF))


def head(ref, i):
    return ref[0, :, i * LANES : (i + 1) * LANES]


def from_vmem(x):
    return pltpu.with_memory_space_constraint(x, pltpu.VMEM)


def from_hbm(x):
    return pltpu.with_memory_space_constraint(x, pltpu.HBM)


class Copies:
    def __init__(self, semaphores):
        self.semaphores = semaphores
        self.used = 0

    def start(self, source, target):
        copy = pltpu.make_async_copy(source, target, self.semaphores.at[self.used])
        self.used += 1
        copy.start()
        return copy


def wait_all(copies):
    for copy in copies:
        copy.wait()


def lanes_of(first, count=1):
    return slice(first * LANES, (first + count) * LANES)


def column(row):
    return jnp.broadcast_to(row, (LANES, LANES)).T


def state_kernel(heads, group, slab, index_hbm, k_hbm, v_hbm, out_hbm, index, k, v, out, semaphores):
    copies = Copies(semaphores)
    index_copy = copies.start(index_hbm, index)
    loads = []
    for first in range(0, heads, group):
        lanes = lanes_of(first, group)
        loads.append([copies.start(x.at[0, :, lanes], y.at[:, lanes]) for x, y in ((k_hbm, k), (v_hbm, v))])
    stores = []
    index_copy.wait()
    for first in range(0, heads, group):
        wait_all(loads[first // group])
        for h in range(first, first + group):
            rate = rate_of(index[h], slab)
            decayed = k[:, lanes_of(h)].astype(F32) * row_powers(rate, slab - 1.0, -1.0, slab)
            out[h] = dot_tn(decayed.astype(BF16), v[:, lanes_of(h)])
        part = slice(first, first + group)
        stores.append(copies.start(out.at[part], out_hbm.at[part]))
    wait_all(stores)


def scan_kernel(slabs, slab, reverse, group, index_ref, place_ref, x_ref, *refs):
    extra, (out_hbm, out, semaphores) = refs[:-3], refs[-3:]
    copies = Copies(semaphores)
    rows = x_ref.shape[1]
    rate = rate_of(index_ref[(place_ref[0] * rows) // LANES], slab)
    factor = jnp.exp2(-rate * float(slab))
    running = jnp.zeros(x_ref.shape[1:], F32)
    order = list(reversed(range(slabs))) if reverse else list(range(slabs))
    stores = []
    for at in range(0, slabs, group):
        for j in order[at : at + group]:
            out[j, :rows] = running
            if extra:
                out[j, rows:] = extra[0][...]
            running = factor * running + x_ref[j]
        part = slice(min(order[at : at + group]), max(order[at : at + group]) + 1)
        stores.append(copies.start(out.at[part], out_hbm.at[part]))
    wait_all(stores)


def local_kernel(
    per_step, slab, total, index_ref, place_ref, length_ref, advantage_ref, q_ref, k_ref, v_ref, mask_ref, imp_ref,
    out_ref, weight_ref,
):
    @pl.when(pl.program_id(0) == 0)
    def _():
        at = place_ref[0] * slab + lax.broadcasted_iota(jnp.int32, (1, slab), 1)
        inside = (at < length_ref[0]).astype(F32)
        length = jnp.full((1, slab), length_ref[0].astype(F32), F32)
        weight = mask_ref[...].astype(F32) * inside * jnp.minimum(imp_ref[...], clip_high)
        weight = weight * advantage_ref[0] * (float(total) / length)
        for b in range(slab // LANES):
            weight_ref[b : b + 1, :] = weight[:, lanes_of(b)]

    for i in range(per_step):
        rate = rate_of(index_ref[pl.program_id(0) * per_step + i], slab)
        diagonal, below = decay_blocks(rate, False)
        q, k, v = head(q_ref, i), head(k_ref, i), head(v_ref, i)
        lanes = lanes_of(i)
        for r in range(slab // HALF):
            scores = dot_nt(q[r * HALF : (r + 1) * HALF], k[: (r + 1) * HALF])
            table = diagonal if r == 0 else jnp.concatenate([below, diagonal], axis=1)
            probs = (scores * table).astype(BF16)
            out_ref[r * HALF : (r + 1) * HALF, lanes] = dot_nn(probs, v[: (r + 1) * HALF])


def output_kernel(
    heads, slab, index_hbm, q_hbm, s_ref, local, c_hbm, weight_ref, gain_hbm, out, q, grad_n, stat_ref,
    index, gain, c, s, semaphores,
):
    copies = Copies(semaphores)
    small = [copies.start(index_hbm, index), copies.start(gain_hbm, gain)]
    loads = []
    for b in range(slab // LANES):
        rows = lanes_of(b)
        loads.append([
            copies.start(q_hbm.at[0, rows], q.at[rows]),
            copies.start(c_hbm.at[0, rows], c.at[rows]),
        ])
    for h in range(heads):
        s[h] = s_ref[h].astype(BF16)
    wait_all(small)
    square_rows, cross_rows = [], []
    for b in range(slab // LANES):
        rows = lanes_of(b)
        weight = column(weight_ref[b : b + 1, :])
        squares = jnp.zeros((LANES, LANES), F32)
        crosses = jnp.zeros((LANES, LANES), F32)
        wait_all(loads[b])
        for h in range(heads):
            rate = rate_of(index[h], slab)
            lanes = lanes_of(h)
            carried = dot_nn(q[rows, lanes], s[h])
            o = local[rows, lanes] + carried * row_powers(rate, b * LANES + 1.0, 1.0, LANES)
            out[rows, lanes] = o
            squares += o * o
            grad = c[rows, lanes].astype(F32) * weight * gain[:, lanes]
            grad_n[rows, lanes] = grad
            crosses += grad * o
        square_rows.append(jnp.sum(squares.T, axis=0, keepdims=True))
        cross_rows.append(jnp.sum(crosses.T, axis=0, keepdims=True))
    stats = jnp.concatenate(square_rows + cross_rows, axis=0)
    for d in range(stat_ref.shape[0]):
        stat_ref[d] = stats


def grad_kernel(
    heads, group, slab, features, index_hbm, stat_ref, q, o, grad_n,
    g_hbm, o_hbm, ret_hbm, inv_ref, index, g, ret, inv_col, mean_col, semaphores,
):
    copies = Copies(semaphores)
    index_copy = copies.start(index_hbm, index)
    stores = [copies.start(o, o_hbm)]
    stats = jnp.sum(stat_ref[...], axis=0)
    blocks = slab // LANES
    inverse = lax.rsqrt(stats[:blocks] / features + epsilon)
    mean = stats[blocks : 2 * blocks] * inverse / features * (inverse * inverse)
    inv_ref[...] = inverse
    for b in range(blocks):
        rows = lanes_of(b)
        inv_col[rows, :] = column(inverse[b : b + 1])
        mean_col[rows, :] = column(mean[b : b + 1])
    index_copy.wait()
    for first in range(0, heads, group):
        for h in range(first, first + group):
            rate = rate_of(index[h], slab)
            lanes = lanes_of(h)
            grad_out = (inv_col[...] * grad_n[:, lanes] - o[:, lanes] * mean_col[...]).astype(BF16)
            g[:, lanes] = grad_out
            decayed = q[:, lanes].astype(F32) * row_powers(rate, 0.0, 1.0, slab)
            ret[h] = dot_tn(decayed.astype(BF16), grad_out)
        part = slice(first, first + group)
        lanes = lanes_of(first, group)
        stores.append(copies.start(ret.at[part], ret_hbm.at[part]))
        stores.append(copies.start(g.at[:, lanes], g_hbm.at[:, lanes]))
    wait_all(stores)


def query_grad_kernel(
    per_step, slab, index_ref, k_ref, v_ref, g_ref, s_ref, o_ref, c_ref, inv_ref, weight_ref,
    qg_ref, gain_out_ref, scale_col,
):
    step = pl.program_id(0)

    @pl.when(step == 0)
    def _():
        for b in range(slab // LANES):
            scale_col[lanes_of(b), :] = column(inv_ref[b : b + 1, :] * weight_ref[b : b + 1, :])

    for i in range(per_step):
        rate = rate_of(index_ref[step * per_step + i], slab)
        lanes = lanes_of(i)
        products = head(c_ref, i).astype(F32) * (o_ref[:, lanes] * scale_col[...])
        gain_out_ref[pl.ds(step * per_step + i, 1), :] = jnp.sum(products, axis=0, keepdims=True)
        k, v, g = head(k_ref, i), head(v_ref, i), g_ref[:, lanes]
        diagonal, below = decay_blocks(rate, False)
        carried = dot_nt(g, s_ref[i].astype(BF16)) * row_powers(rate, 1.0, 1.0, slab)
        a, b = slice(0, HALF), slice(HALF, 2 * HALF)
        upper = (dot_nt(g[a], v[a]) * diagonal).astype(BF16)
        lower = (dot_nt(g[b], v) * jnp.concatenate([below, diagonal], axis=1)).astype(BF16)
        qg_ref[0, a, lanes] = (dot_nn(upper, k[a]) + carried[a]).astype(BF16)
        qg_ref[0, b, lanes] = (dot_nn(lower, k) + carried[b]).astype(BF16)


def key_value_kernel(
    per_step, slab, index_ref, q_ref, k_ref, v_ref, g_ref, o_ref, inv_ref, gain_ref, mixed_ref, kl_ref, vl_ref, inv_col
):
    @pl.when(pl.program_id(0) == 0)
    def _():
        for b in range(slab // LANES):
            inv_col[lanes_of(b), :] = column(inv_ref[b : b + 1, :])

    for i in range(per_step):
        mixed_ref[0, :, lanes_of(i)] = (o_ref[:, lanes_of(i)] * inv_col[...] * gain_ref[:, lanes_of(i)]).astype(BF16)
        rate = rate_of(index_ref[pl.program_id(0) * per_step + i], slab)
        lanes = lanes_of(i)
        q, k, v, g = head(q_ref, i), head(k_ref, i), head(v_ref, i), g_ref[:, lanes]
        diagonal, below = decay_blocks(rate, True)
        a, b = slice(0, HALF), slice(HALF, 2 * HALF)
        table = jnp.concatenate([diagonal, below], axis=1)
        for x, y, z, ref in ((v, g, q, kl_ref), (k, q, g, vl_ref)):
            first = (dot_nt(x[a], y) * table).astype(BF16)
            second = (dot_nt(x[b], y[b]) * diagonal).astype(BF16)
            ref[a, lanes] = dot_nn(first, z).astype(BF16)
            ref[b, lanes] = dot_nn(second, z[b]).astype(BF16)


def final_kernel(
    heads, group, slab, size, index_hbm, r_ref, k_hbm, v_hbm, kl, vl, kg_hbm, vg_hbm, index, k, v, kg, vg, semaphores
):
    copies = Copies(semaphores)
    index_copy = copies.start(index_hbm, index)
    loads = []
    for first in range(0, heads, group):
        lanes = lanes_of(first, group)
        loads.append([copies.start(x.at[0, :, lanes], y.at[:, lanes]) for x, y in ((k_hbm, k), (v_hbm, v))])
    pieces = LANES // size
    index_copy.wait()
    stores = []
    for first in range(0, heads, group):
        wait_all(loads[first // group])
        for h in range(first, first + group):
            lanes = lanes_of(h)
            to_next = row_powers(rate_of(index[h], slab), float(slab), -1.0, slab)
            back = jnp.concatenate([r_ref[h * pieces + p, :size] for p in range(pieces)], axis=0).astype(BF16)
            kg[:, lanes] = (kl[:, lanes].astype(F32) + dot_nt(v[:, lanes], back) * to_next).astype(BF16)
            vg[:, lanes] = (vl[:, lanes].astype(F32) + dot_nn(k[:, lanes], back) * to_next).astype(BF16)
        lanes = lanes_of(first, group)
        stores += [copies.start(x.at[:, lanes], y.at[0, :, lanes]) for x, y in ((kg, kg_hbm), (vg, vg_hbm))]
    wait_all(stores)


def on_device(query_rows, key_rows, value_rows, norm_gain, cotangent, loss_mask, importance, advantage, lengths, decay_index):
    _, slab, features = query_rows.shape
    heads = decay_index.shape[0]
    slabs = lax.axis_size("seq")
    place = lax.axis_index("seq").reshape(1)
    size = heads * LANES // slabs
    total_features = float(features * lax.axis_size("head"))
    per_step = 2
    steps = heads // per_step
    wide = per_step * LANES
    blocks = slab // LANES
    gain_row = from_hbm(norm_gain.reshape(1, features))
    decay_hbm, query, key, value, upstream = map(from_hbm, (decay_index, query_rows, key_rows, value_rows, cotangent))

    smem = pl.BlockSpec(memory_space=pltpu.SMEM)
    vmem = pl.BlockSpec(memory_space=pltpu.VMEM)
    anywhere = pl.BlockSpec(memory_space=pl.ANY)
    token = pl.BlockSpec((1, slab, wide), lambda i: (0, 0, i))
    flat = pl.BlockSpec((slab, wide), lambda i: (0, i))
    gain_spec = pl.BlockSpec((1, wide), lambda i: (0, i))
    state = pl.BlockSpec((per_step, LANES, LANES), lambda i: (i, 0, 0))
    token_row = pl.BlockSpec((blocks, LANES), lambda i: (0, 0))
    gain_out = pl.BlockSpec((heads, LANES), lambda i: (0, 0))
    token_f32 = pltpu.HBM((slab, features), F32)
    token_out = pltpu.HBM(query_rows.shape, BF16)
    state_out = pltpu.HBM((heads, LANES, LANES), F32)
    row_out = jax.ShapeDtypeStruct((blocks, LANES), F32)
    gain_f32 = jax.ShapeDtypeStruct((heads, LANES), F32)
    params = pltpu.CompilerParams(vmem_limit_bytes=24 * 1024 * 1024)

    def held(dtype):
        return pltpu.VMEM((slab, features), dtype)

    def semaphores(count):
        return pltpu.SemaphoreType.DMA((count,))

    index_held = pltpu.SMEM((heads,), jnp.int32)
    gain_held = pltpu.VMEM((1, features), F32)
    state_held = pltpu.VMEM((heads, LANES, LANES), F32)
    state_half = pltpu.VMEM((heads, LANES, LANES), BF16)
    columns = pltpu.VMEM((slab, LANES), F32)

    def over_slabs(pieces):
        return lax.all_to_all(pieces, "seq", 0, 0, tiled=True)

    group = 2
    state_local = pl.pallas_call(
        functools.partial(state_kernel, heads, group, slab),
        in_specs=[anywhere] * 3,
        out_specs=anywhere,
        out_shape=state_out,
        scratch_shapes=[index_held, held(BF16), held(BF16), state_held, semaphores(1 + 3 * heads // group)],
        compiler_params=params,
        name="state_local",
    )(decay_hbm, key, value)
    sent = over_slabs(state_local.reshape(slabs, size, LANES))

    local_out, weight = pl.pallas_call(
        functools.partial(local_kernel, per_step, slab, slab * slabs),
        grid=(steps,),
        in_specs=[smem, smem, smem, smem, token, token, token]
        + [pl.BlockSpec((1, slab), lambda i: (0, 0))] * 2,
        out_specs=[flat, token_row],
        out_shape=[pltpu.VMEM((slab, features), F32), row_out],
        compiler_params=params,
        name="local_attention",
    )(decay_index, place, lengths, advantage, query, key, value, loss_mask, importance)
    local_out = from_vmem(local_out)

    def scan(reverse, pieces, extra, name):
        shape = (slabs, size + (heads if extra else 0), LANES)
        return pl.pallas_call(
            functools.partial(scan_kernel, slabs, slab, reverse, 4),
            in_specs=[smem, smem, vmem] + [vmem] * len(extra),
            out_specs=anywhere,
            out_shape=pltpu.HBM(shape, F32),
            scratch_shapes=[pltpu.VMEM(shape, F32), semaphores(slabs // 4)],
            compiler_params=params,
            name=name,
        )(decay_index, place, pieces, *extra)

    state_in = over_slabs(scan(False, sent, (), "prefix")).reshape(heads, LANES, LANES)

    groups = lax.axis_size("head")
    outputs, query_held, grad_n, stats = pl.pallas_call(
        functools.partial(output_kernel, heads, slab),
        in_specs=[anywhere, anywhere, vmem, vmem, anywhere, vmem, anywhere],
        out_specs=[vmem] * 4,
        out_shape=[held(F32), held(BF16), held(F32), jax.ShapeDtypeStruct((groups, 2 * blocks, LANES), F32)],
        scratch_shapes=[index_held, gain_held, held(BF16), state_half, semaphores(2 + 2 * blocks)],
        compiler_params=params,
        name="outputs",
    )(decay_hbm, query, state_in, local_out, upstream, weight, gain_row)
    stats = lax.all_to_all(stats, "head", 0, 0, tiled=True)

    grad_out, outputs, return_local, inverse = pl.pallas_call(
        functools.partial(grad_kernel, heads, group, slab, total_features),
        in_specs=[anywhere, vmem, vmem, vmem, vmem],
        out_specs=[anywhere, anywhere, anywhere, vmem],
        out_shape=[pltpu.HBM((slab, features), BF16), token_f32, state_out, row_out],
        scratch_shapes=[
            index_held, held(BF16), state_held, columns, columns, semaphores(2 + 2 * heads // group)
        ],
        compiler_params=params,
        name="output_grad",
    )(decay_hbm, stats, from_vmem(query_held), from_vmem(outputs), from_vmem(grad_n))
    grad_out, outputs = from_hbm(grad_out), from_hbm(outputs)
    returned = over_slabs(return_local.reshape(slabs, size, LANES))

    query_grad, gain_part = pl.pallas_call(
        functools.partial(query_grad_kernel, per_step, slab),
        grid=(steps,),
        in_specs=[smem, token, token, flat, state, flat, token, token_row, token_row],
        out_specs=[token, gain_out],
        out_shape=[token_out, gain_f32],
        scratch_shapes=[columns],
        compiler_params=params,
        name="query_grads",
    )(decay_index, key, value, grad_out, state_in, outputs, upstream, inverse, weight)
    return_in = over_slabs(scan(True, returned, (gain_part,), "suffix"))

    mixed, key_local, value_local = pl.pallas_call(
        functools.partial(key_value_kernel, per_step, slab),
        grid=(steps,),
        in_specs=[smem, token, token, token, flat, flat, token_row, gain_spec],
        out_specs=[token, flat, flat],
        out_shape=[token_out, held(BF16), held(BF16)],
        scratch_shapes=[columns],
        compiler_params=params,
        name="key_value_grads",
    )(decay_index, query, key, value, grad_out, outputs, inverse, gain_row)

    return_in, key_local, value_local = lax.optimization_barrier((return_in, key_local, value_local))
    gain_sum = jnp.sum(return_in[:, size:], axis=0)
    other_sum = lax.ppermute(gain_sum, "dp", [(i, 1 - i) for i in range(2)])
    key_grad, value_grad = pl.pallas_call(
        functools.partial(final_kernel, heads, group, slab, size),
        in_specs=[anywhere, vmem, anywhere, anywhere, vmem, vmem],
        out_specs=[anywhere, anywhere],
        out_shape=[token_out, token_out],
        scratch_shapes=[index_held] + [held(BF16)] * 4 + [semaphores(1 + 4 * heads // group)],
        compiler_params=params,
        name="final_grads",
    )(decay_hbm, return_in, key, value, from_vmem(key_local), from_vmem(value_local))
    gain_grad = (gain_sum + other_sum).reshape(features)
    return (mixed, query_grad, key_grad, value_grad, gain_grad)


def solution(mesh):
    tokens = P("dp", "seq", "head")
    return jax.shard_map(
        on_device,
        mesh=mesh,
        in_specs=(
            tokens, tokens, tokens, P("head"), tokens, P("dp", "seq"), P("dp", "seq"), P("dp"), P("dp"), P("head"),
        ),
        out_specs=(tokens, tokens, tokens, tokens, P("head")),
        check_vma=False,
    )
```

time: 107 us -> 95.6 us (0.89)
  the two profiles are of different devices: /device:TPU:2 before, /device:TPU:1 now
where the time goes in v2:
time: 95.6 us; the launch traced here: 94.8 us
  Pallas kernels  33.7 us (35%)
  starting transfers between devices  24.8 us (26%)
  waiting for transfers between devices  18.7 us (20%)
  blocking collectives  14.9 us (16%)
  between operations  2.08 us (2%)
    all_to_all x4, waiting for transfers between devices, over_slabs(): return lax.all_to_all(pieces, 'seq', 0, 0, tiled=True)  18.7 us
    all_to_all x4, starting transfers between devices, over_slabs(): return lax.all_to_all(pieces, 'seq', 0, 0, tiled=True)  18.4 us
    all_to_all x1, blocking collectives, on_device(): stats = lax.all_to_all(stats, 'head', 0, 0, tiled=True)  14.9 us
    pallas_call x1, Pallas kernels, on_device(): pl.pallas_call(functools.partial(key_value_kernel, per_step, slab), grid=...  7.28 us
    ppermute x1, starting transfers between devices, on_device(): other_sum = lax.ppermute(gain_sum, 'dp', [(i, 1 - i) for i in range(2)])  6.41 us
    pallas_call x1, Pallas kernels, on_device(): pl.pallas_call(functools.partial(query_grad_kernel, per_step, slab), grid...  6.07 us
    pallas_call x1, Pallas kernels, on_device(): pl.pallas_call(functools.partial(local_kernel, per_step, slab, slab * sla...  5.2 us
    pallas_call x1, Pallas kernels, on_device(): pl.pallas_call(functools.partial(final_kernel, heads, group, slab, size),...  3.46 us
  transfers between devices with their start and end apart: 5, of which 4 were waited for; matrix products, arithmetic and copies ran while one was open for 0% of the time, Pallas kernels for 23%

profile of v2, /device:TPU:1, one launch (start us, length us, event | category | flops | bytes accessed | tf_op | source)
XLA Modules:
  0.0 94.8 jit_solution(14818037057113172776)
XLA Ops:
  0.6 0.0 copy-start
  0.6 3.1 %state_local.1 = f32[8,128,128]{2,1,0:T(8,128)} custom-call(s32[8]{0:T(128)} %index_hbm.7, bf16[1,512,1024]{2,1,0:T(8,128)(2,1)} %k_hbm.3, bf16[1,512,1024]{2,1,0:T(8,128)(2,1)} %v_hbm.3), custom_call_target="tpu_custom_call" | custom-call | tf_op jit(solution)/shard_map/state_local/pallas_call | solution.py:345
  3.8 0.0 copy-start.2
  3.8 0.0 copy-start.3
  3.8 7.6 %all-to-all-start = ((f32[16,64,128]{2,1,0:T(8,128)}), f32[16,64,128]{2,1,0:T(8,128)S(1)}, u32[]{:S(2)}, u32[]{:S(2)}) async-start(f32[16,64,128]{2,1,0:T(8,128)} %bitcast.9), calls=%async_computation | async-start | bytes 1048576 | tf_op jit(solution)/shard_map/all_to_all | solution.py:342
  11.4 10.5 %all-to-all-done.x_ref = f32[16,64,128]{2,1,0:T(8,128)S(1)} async-done(((f32[16,64,128]{2,1,0:T(8,128)}), f32[16,64,128]{2,1,0:T(8,128)S(1)}, u32[]{:S(2)}, u32[]{:S(2)}) %all-to-all-start) | async-done | bytes 524320 | tf_op jit(solution)/shard_map/all_to_all | solution.py:342
  21.9 0.0 copy-done
  21.9 1.4 %prefix.1 = f32[16,64,128]{2,1,0:T(8,128)} custom-call(s32[8]{0:T(128)S(1)} %copy-done, s32[1]{0:T(128)} %bitcast.place_ref, f32[16,64,128]{2,1,0:T(8,128)S(1)} %all-to-all-done.x_ref), custom_call_target="tpu_custom_call" | custom-call | tf_op jit(solution)/shard_map/prefix/pallas_call | solution.py:370
  23.3 3.6 %all-to-all-start.1 = ((f32[16,64,128]{2,1,0:T(8,128)}), f32[16,64,128]{2,1,0:T(8,128)S(1)}, u32[]{:S(2)}, u32[]{:S(2)}) async-start(f32[16,64,128]{2,1,0:T(8,128)} %prefix.1), calls=%async_computation.1 | async-start | bytes 1048576 | tf_op jit(solution)/shard_map/all_to_all | solution.py:342
  28.2 0.0 copy-done.2
  28.2 0.0 copy-done.3
  28.2 5.2 %local_attention.1 = (f32[512,1024]{1,0:T(8,128)S(1)}, f32[4,128]{1,0:T(4,128)S(1)}) custom-call(s32[8]{0:T(128)S(1)} %copy-done, s32[1]{0:T(128)} %bitcast.place_ref, s32[1]{0:T(128)S(6)} %copy.16.length_ref, f32[1]{0:T(128)S(6)} %copy.15.advantage_ref, bf16[1,512,1024]{2,1,0:T(8,128)(2,1)} %q_ref.3, bf16[1,512,1024]{2,1,0:T(8,128)(2,1)} %k_hbm.3, ...), custom_call_target="tpu_custom_call" | custom-call | tf_op jit(solution)/shard_map/local_attention/pallas_call | solution.py:356
  33.4 3.1 %all-to-all-done.1 = f32[16,64,128]{2,1,0:T(8,128)S(1)} async-done(((f32[16,64,128]{2,1,0:T(8,128)}), f32[16,64,128]{2,1,0:T(8,128)S(1)}, u32[]{:S(2)}, u32[]{:S(2)}) %all-to-all-start.1) | async-done | bytes 524320 | tf_op jit(solution)/shard_map/all_to_all | solution.py:342
  36.6 2.8 %outputs.1 = (f32[512,1024]{1,0:T(8,128)S(1)}, bf16[512,1024]{1,0:T(8,128)(2,1)S(1)}, f32[512,1024]{1,0:T(8,128)S(1)}, f32[8,8,128]{2,1,0:T(8,128)S(1)}) custom-call(s32[8]{0:T(128)} %index_hbm.7, bf16[1,512,1024]{2,1,0:T(8,128)(2,1)} %q_ref.3, f32[8,128,128]{2,1,0:T(8,128)S(1)} %bitcast.7, f32[512,1024]{1,0:T(8,128)S(1)} %get-tuple-element.25.local, ...), custom_call_target="tpu_custom_call" | custom-call | tf_op jit(solution)/shard_map/outputs/pallas_call | solution.py:383
  39.3 14.9 %all_to_all.25.stat_ref = f32[8,8,128]{2,1,0:T(8,128)S(1)} all-to-all(f32[8,8,128]{2,1,0:T(8,128)S(1)} %get-tuple-element.27), channel_id=1, replica_groups=mesh['dp'=2,'seq'=16,'head'=8] {'head'}, dimensions={0} | all-to-all | bytes 65536 | tf_op jit(solution)/shard_map/all_to_all | solution.py:392
  54.2 0.0 copy-start.1
  54.2 3.0 %output_grad.1 = (bf16[512,1024]{1,0:T(8,128)(2,1)}, f32[512,1024]{1,0:T(8,128)}, f32[8,128,128]{2,1,0:T(8,128)}, f32[4,128]{1,0:T(4,128)S(1)}) custom-call(s32[8]{0:T(128)} %index_hbm.7, f32[8,8,128]{2,1,0:T(8,128)S(1)} %all_to_all.25.stat_ref, bf16[512,1024]{1,0:T(8,128)(2,1)S(1)} %get-tuple-element.28.q, f32[512,1024]{1,0:T(8,128)S(1)} %get-tuple-element.29.o, ...), custom_call_target="tpu_custom_call" | custom-call | tf_op jit(solution)/shard_map/output_grad/pallas_call | solution.py:394
  57.2 3.6 %all-to-all-start.3 = ((f32[16,64,128]{2,1,0:T(8,128)}), f32[16,64,128]{2,1,0:T(8,128)S(1)}, u32[]{:S(2)}, u32[]{:S(2)}) async-start(f32[16,64,128]{2,1,0:T(8,128)} %bitcast.10), calls=%async_computation.3 | async-start | bytes 1048576 | tf_op jit(solution)/shard_map/all_to_all | solution.py:342
  60.8 0.0 copy-done.1
  60.8 6.1 %query_grads.1 = (bf16[1,512,1024]{2,1,0:T(8,128)(2,1)}, f32[8,128]{1,0:T(8,128)S(1)}) custom-call(s32[8]{0:T(128)S(1)} %copy-done.1, bf16[1,512,1024]{2,1,0:T(8,128)(2,1)} %k_hbm.3, bf16[1,512,1024]{2,1,0:T(8,128)(2,1)} %v_hbm.3, bf16[512,1024]{1,0:T(8,128)(2,1)} %get-tuple-element.31.g_ref, f32[8,128,128]{2,1,0:T(8,128)S(1)} %bitcast.8, ...), custom_call_target="tpu_custom_call" | custom-call | tf_op jit(solution)/shard_map/query_grads/pallas_call | solution.py:408
  66.9 3.0 %all-to-all-done.3.x_ref = f32[16,64,128]{2,1,0:T(8,128)S(1)} async-done(((f32[16,64,128]{2,1,0:T(8,128)}), f32[16,64,128]{2,1,0:T(8,128)S(1)}, u32[]{:S(2)}, u32[]{:S(2)}) %all-to-all-start.3) | async-done | bytes 524320 | tf_op jit(solution)/shard_map/all_to_all | solution.py:342
  69.9 1.4 %suffix.1 = f32[16,72,128]{2,1,0:T(8,128)} custom-call(s32[8]{0:T(128)S(1)} %copy-done.1, s32[1]{0:T(128)} %bitcast.place_ref, f32[16,64,128]{2,1,0:T(8,128)S(1)} %all-to-all-done.3.x_ref, f32[8,128]{1,0:T(8,128)S(1)} %get-tuple-element.37.refs_0_), custom_call_target="tpu_custom_call" | custom-call | tf_op jit(solution)/shard_map/suffix/pallas_call | solution.py:370
  71.3 3.7 %all-to-all-start.4 = ((f32[16,72,128]{2,1,0:T(8,128)}), f32[16,72,128]{2,1,0:T(8,128)S(1)}, u32[]{:S(2)}, u32[]{:S(2)}) async-start(f32[16,72,128]{2,1,0:T(8,128)} %suffix.1), calls=%async_computation.4 | async-start | bytes 1179648 | tf_op jit(solution)/shard_map/all_to_all | solution.py:342
  75.0 7.3 %key_value_grads.1 = (bf16[1,512,1024]{2,1,0:T(8,128)(2,1)}, bf16[512,1024]{1,0:T(8,128)(2,1)S(1)}, bf16[512,1024]{1,0:T(8,128)(2,1)S(1)}) custom-call(s32[8]{0:T(128)S(1)} %copy-done.1, bf16[1,512,1024]{2,1,0:T(8,128)(2,1)} %q_ref.3, bf16[1,512,1024]{2,1,0:T(8,128)(2,1)} %k_hbm.3, bf16[1,512,1024]{2,1,0:T(8,128)(2,1)} %v_hbm.3, ...), custom_call_target="tpu_custom_call" | custom-call | tf_op jit(solution)/shard_map/key_value_grads/pallas_call | solution.py:420
  82.2 2.1 %all-to-all-done.4.r_ref = f32[16,72,128]{2,1,0:T(8,128)S(1)} async-done(((f32[16,72,128]{2,1,0:T(8,128)}), f32[16,72,128]{2,1,0:T(8,128)S(1)}, u32[]{:S(2)}, u32[]{:S(2)}) %all-to-all-start.4) | async-done | bytes 589856 | tf_op jit(solution)/shard_map/all_to_all | solution.py:342
  84.3 6.4 %collective-permute-start = (f32[8,128]{1,0:T(8,128)S(1)}, f32[8,128]{1,0:T(8,128)S(1)}, u32[]{:S(2)}, u32[]{:S(2)}) collective-permute-start(f32[8,128]{1,0:T(8,128)S(1)} %slice_reduce_fusion), channel_id=1, source_target_pairs={{0,128},{128,0},{1,129},{129,1},{2,130},{130,2},{3,131},{131,3},{4... | collective-permute-start | bytes 12296 | tf_op jit(solution)/shard_map/ppermute | solution.py:433
  90.7 3.5 %final_grads.1 = (bf16[1,512,1024]{2,1,0:T(8,128)(2,1)}, bf16[1,512,1024]{2,1,0:T(8,128)(2,1)}) custom-call(s32[8]{0:T(128)} %index_hbm.7, f32[16,72,128]{2,1,0:T(8,128)S(1)} %all-to-all-done.4.r_ref, bf16[1,512,1024]{2,1,0:T(8,128)(2,1)} %k_hbm.3, bf16[1,512,1024]{2,1,0:T(8,128)(2,1)} %v_hbm.3, bf16[512,1024]{1,0:T(8,128)(2,1)S(1)} %get-tuple-element.41.kl, ...), custom_call_target="tpu_custom_call" | custom-call | tf_op jit(solution)/shard_map/final_grads/pallas_call | solution.py:434
  94.2 0.0 collective-permute-done
  94.2 0.6 add_bitcast_fusion
  (1 shorter events, 0.0 us)
Async XLA Ops:
  0.6 21.3 %copy-start = (s32[8]{0:T(128)S(1)}, s32[8]{0:T(128)}, u32[]{:S(2)}) copy-start(s32[8]{0:T(128)} %index_hbm.7) | copy-start | bytes 100
  3.8 24.4 %copy-start.2 = (s32[1,512]{1,0:T(1,128)S(1)}, s32[1,512]{1,0:T(1,128)}, u32[]{:S(2)}) copy-start(s32[1,512]{1,0:T(1,128)} %mask_ref.1) | copy-start | bytes 6148
  3.8 24.4 %copy-start.3 = (f32[1,512]{1,0:T(1,128)S(1)}, f32[1,512]{1,0:T(1,128)}, u32[]{:S(2)}) copy-start(f32[1,512]{1,0:T(1,128)} %imp_ref.1) | copy-start | bytes 6148
  3.8 18.1 %all-to-all-start = ((f32[16,64,128]{2,1,0:T(8,128)}), f32[16,64,128]{2,1,0:T(8,128)S(1)}, u32[]{:S(2)}, u32[]{:S(2)}) async-start(f32[16,64,128]{2,1,0:T(8,128)} %bitcast.9), calls=%async_computation | async-start | bytes 1048576 | tf_op jit(solution)/shard_map/all_to_all | solution.py:342
  23.3 13.3 %all-to-all-start.1 = ((f32[16,64,128]{2,1,0:T(8,128)}), f32[16,64,128]{2,1,0:T(8,128)S(1)}, u32[]{:S(2)}, u32[]{:S(2)}) async-start(f32[16,64,128]{2,1,0:T(8,128)} %prefix.1), calls=%async_computation.1 | async-start | bytes 1048576 | tf_op jit(solution)/shard_map/all_to_all | solution.py:342
  54.2 6.6 %copy-start.1 = (s32[8]{0:T(128)S(1)}, s32[8]{0:T(128)}, u32[]{:S(2)}) copy-start(s32[8]{0:T(128)} %index_hbm.7) | copy-start | bytes 100
  57.2 12.7 %all-to-all-start.3 = ((f32[16,64,128]{2,1,0:T(8,128)}), f32[16,64,128]{2,1,0:T(8,128)S(1)}, u32[]{:S(2)}, u32[]{:S(2)}) async-start(f32[16,64,128]{2,1,0:T(8,128)} %bitcast.10), calls=%async_computation.3 | async-start | bytes 1048576 | tf_op jit(solution)/shard_map/all_to_all | solution.py:342
  71.3 13.0 %all-to-all-start.4 = ((f32[16,72,128]{2,1,0:T(8,128)}), f32[16,72,128]{2,1,0:T(8,128)S(1)}, u32[]{:S(2)}, u32[]{:S(2)}) async-start(f32[16,72,128]{2,1,0:T(8,128)} %suffix.1), calls=%async_computation.4 | async-start | bytes 1179648 | tf_op jit(solution)/shard_map/all_to_all | solution.py:342
  84.3 9.9 %collective-permute-start = (f32[8,128]{1,0:T(8,128)S(1)}, f32[8,128]{1,0:T(8,128)S(1)}, u32[]{:S(2)}, u32[]{:S(2)}) collective-permute-start(f32[8,128]{1,0:T(8,128)S(1)} %slice_reduce_fusion), channel_id=1, source_target_pairs={{0,128},{128,0},{1,129},{129,1},{2,130},{130,2},{3,131},{131,3},{4... | collective-permute-start | bytes 12296 | tf_op jit(solution)/shard_map/ppermute | solution.py:433

commit v3 on v2

--- a/solution.py
+++ b/solution.py
@@ -84,43 +84,45 @@
     return jnp.broadcast_to(row, (LANES, LANES)).T
 
 
-def state_kernel(heads, group, slab, index_hbm, k_hbm, v_hbm, out_hbm, index, k, v, out, semaphores):
+def state_kernel(heads, slab, index_hbm, k_hbm, v_hbm, out_hbm, index, k, v, out, semaphores):
     copies = Copies(semaphores)
     index_copy = copies.start(index_hbm, index)
-    loads = []
-    for first in range(0, heads, group):
-        lanes = lanes_of(first, group)
-        loads.append([copies.start(x.at[0, :, lanes], y.at[:, lanes]) for x, y in ((k_hbm, k), (v_hbm, v))])
+    spans = [slice(at, at + HALF) for at in range(0, slab, HALF)]
+    loads = [[copies.start(x.at[0, rows], y.at[rows]) for x, y in ((k_hbm, k), (v_hbm, v))] for rows in spans]
     stores = []
     index_copy.wait()
-    for first in range(0, heads, group):
-        wait_all(loads[first // group])
-        for h in range(first, first + group):
-            rate = rate_of(index[h], slab)
-            decayed = k[:, lanes_of(h)].astype(F32) * row_powers(rate, slab - 1.0, -1.0, slab)
-            out[h] = dot_tn(decayed.astype(BF16), v[:, lanes_of(h)])
-        part = slice(first, first + group)
-        stores.append(copies.start(out.at[part], out_hbm.at[part]))
+    for rows, load in zip(spans, loads):
+        wait_all(load)
+        for h in range(heads):
+            powers = row_powers(rate_of(index[h], slab), slab - 1.0 - rows.start, -1.0, HALF)
+            decayed = (k[rows, lanes_of(h)].astype(F32) * powers).astype(BF16)
+            term = dot_tn(decayed, v[rows, lanes_of(h)])
+            out[h] = term if rows.start == 0 else out[h] + term
+            if rows.stop == slab and h % 4 == 3:
+                part = slice(h - 3, h + 1)
+                stores.append(copies.start(out.at[part], out_hbm.at[part]))
     wait_all(stores)
 
 
-def scan_kernel(slabs, slab, reverse, group, index_ref, place_ref, x_ref, *refs):
-    extra, (out_hbm, out, semaphores) = refs[:-3], refs[-3:]
+def scan_kernel(slabs, slab, size, reverse, group, index_ref, place_ref, x_ref, out_hbm, *refs):
+    extra, (out, semaphores) = refs[:-2], refs[-2:]
     copies = Copies(semaphores)
-    rows = x_ref.shape[1]
-    rate = rate_of(index_ref[(place_ref[0] * rows) // LANES], slab)
+    rate = rate_of(index_ref[(place_ref[0] * size) // LANES], slab)
     factor = jnp.exp2(-rate * float(slab))
-    running = jnp.zeros(x_ref.shape[1:], F32)
+    running = jnp.zeros((size, LANES), F32)
     order = list(reversed(range(slabs))) if reverse else list(range(slabs))
     stores = []
     for at in range(0, slabs, group):
         for j in order[at : at + group]:
-            out[j, :rows] = running
-            if extra:
-                out[j, rows:] = extra[0][...]
-            running = factor * running + x_ref[j]
+            out[j] = running
+            running = factor * running + x_ref[j, :size]
         part = slice(min(order[at : at + group]), max(order[at : at + group]) + 1)
         stores.append(copies.start(out.at[part], out_hbm.at[part]))
+    if extra:
+        total = x_ref[0, size:]
+        for j in range(1, slabs):
+            total += x_ref[j, size:]
+        extra[0][...] = total
     wait_all(stores)
 
 
@@ -151,14 +153,15 @@
 
 
 def output_kernel(
-    heads, slab, index_hbm, q_hbm, s_ref, local, c_hbm, weight_ref, gain_hbm, out, q, grad_n, stat_ref,
+    heads, slab, index_hbm, q_hbm, s_ref, local, c_hbm, weight_ref, gain_hbm, out, q, grad_y, stat_ref,
     index, gain, c, s, semaphores,
 ):
     copies = Copies(semaphores)
     small = [copies.start(index_hbm, index), copies.start(gain_hbm, gain)]
     loads = []
-    for b in range(slab // LANES):
-        rows = lanes_of(b)
+    span = HALF // LANES
+    for b in range(0, slab // LANES, span):
+        rows = lanes_of(b, span)
         loads.append([
             copies.start(q_hbm.at[0, rows], q.at[rows]),
             copies.start(c_hbm.at[0, rows], c.at[rows]),
@@ -167,77 +170,87 @@
         s[h] = s_ref[h].astype(BF16)
     wait_all(small)
     square_rows, cross_rows = [], []
-    for b in range(slab // LANES):
-        rows = lanes_of(b)
-        weight = column(weight_ref[b : b + 1, :])
-        squares = jnp.zeros((LANES, LANES), F32)
-        crosses = jnp.zeros((LANES, LANES), F32)
-        wait_all(loads[b])
+    for b in range(0, slab // LANES, span):
+        rows = lanes_of(b, span)
+        weight = jnp.concatenate([column(weight_ref[x : x + 1, :]) for x in range(b, b + span)], axis=0)
+        squares = jnp.zeros((HALF, LANES), F32)
+        crosses = jnp.zeros((HALF, LANES), F32)
+        wait_all(loads[b // span])
         for h in range(heads):
             rate = rate_of(index[h], slab)
             lanes = lanes_of(h)
             carried = dot_nn(q[rows, lanes], s[h])
-            o = local[rows, lanes] + carried * row_powers(rate, b * LANES + 1.0, 1.0, LANES)
+            o = local[rows, lanes] + carried * row_powers(rate, b * LANES + 1.0, 1.0, HALF)
             out[rows, lanes] = o
             squares += o * o
-            grad = c[rows, lanes].astype(F32) * weight * gain[:, lanes]
-            grad_n[rows, lanes] = grad
-            crosses += grad * o
-        square_rows.append(jnp.sum(squares.T, axis=0, keepdims=True))
-        cross_rows.append(jnp.sum(crosses.T, axis=0, keepdims=True))
+            grad = c[rows, lanes].astype(F32) * weight
+            grad_y[rows, lanes] = grad
+            crosses += (grad * gain[:, lanes]) * o
+        for x in range(span):
+            square_rows.append(jnp.sum(squares[lanes_of(x)].T, axis=0, keepdims=True))
+            cross_rows.append(jnp.sum(crosses[lanes_of(x)].T, axis=0, keepdims=True))
     stats = jnp.concatenate(square_rows + cross_rows, axis=0)
     for d in range(stat_ref.shape[0]):
         stat_ref[d] = stats
 
 
 def grad_kernel(
-    heads, group, slab, features, index_hbm, stat_ref, q, o, grad_n,
-    g_hbm, o_hbm, ret_hbm, inv_ref, index, g, ret, inv_col, mean_col, semaphores,
+    heads, group, slab, features, size, index_hbm, stat_ref, q, o, grad_y, gain_hbm,
+    g_hbm, o_hbm, ret_hbm, inv_ref, index, gain, g, ret, inv_col, mean_col, semaphores,
 ):
     copies = Copies(semaphores)
-    index_copy = copies.start(index_hbm, index)
+    small = [copies.start(index_hbm, index), copies.start(gain_hbm, gain)]
     stores = [copies.start(o, o_hbm)]
     stats = jnp.sum(stat_ref[...], axis=0)
     blocks = slab // LANES
     inverse = lax.rsqrt(stats[:blocks] / features + epsilon)
-    mean = stats[blocks : 2 * blocks] * inverse / features * (inverse * inverse)
+    mean = stats[blocks : 2 * blocks] * inverse / features
     inv_ref[...] = inverse
     for b in range(blocks):
         rows = lanes_of(b)
         inv_col[rows, :] = column(inverse[b : b + 1])
         mean_col[rows, :] = column(mean[b : b + 1])
-    index_copy.wait()
+    wait_all(small)
+    pieces = LANES // size
+    gain_rows = []
     for first in range(0, heads, group):
         for h in range(first, first + group):
             rate = rate_of(index[h], slab)
             lanes = lanes_of(h)
-            grad_out = (inv_col[...] * grad_n[:, lanes] - o[:, lanes] * mean_col[...]).astype(BF16)
+            normed = o[:, lanes] * inv_col[...]
+            gain_rows.append(jnp.sum(grad_y[:, lanes] * normed, axis=0, keepdims=True))
+            grad_n = grad_y[:, lanes] * gain[:, lanes]
+            grad_out = (inv_col[...] * (grad_n - normed * mean_col[...])).astype(BF16)
             g[:, lanes] = grad_out
             decayed = q[:, lanes].astype(F32) * row_powers(rate, 0.0, 1.0, slab)
-            ret[h] = dot_tn(decayed.astype(BF16), grad_out)
-        part = slice(first, first + group)
+            local = dot_tn(decayed.astype(BF16), grad_out)
+            for p in range(pieces):
+                ret[h * pieces + p, :size] = local[p * size : (p + 1) * size]
+        part = slice(first * pieces, (first + group) * pieces)
         lanes = lanes_of(first, group)
-        stores.append(copies.start(ret.at[part], ret_hbm.at[part]))
+        stores.append(copies.start(ret.at[part, :size], ret_hbm.at[part, :size]))
         stores.append(copies.start(g.at[:, lanes], g_hbm.at[:, lanes]))
+    gains = jnp.concatenate(gain_rows, axis=0)
+    for j in range(heads * pieces):
+        ret[j, size:] = gains
+    stores.append(copies.start(ret.at[:, size:], ret_hbm.at[:, size:]))
     wait_all(stores)
 
 
 def query_grad_kernel(
-    per_step, slab, index_ref, k_ref, v_ref, g_ref, s_ref, o_ref, c_ref, inv_ref, weight_ref,
-    qg_ref, gain_out_ref, scale_col,
+    per_step, slab, index_ref, k_ref, v_ref, g_ref, s_ref, o_ref, inv_ref, gain_ref, mixed_ref, qg_ref, inv_col
 ):
     step = pl.program_id(0)
 
     @pl.when(step == 0)
     def _():
         for b in range(slab // LANES):
-            scale_col[lanes_of(b), :] = column(inv_ref[b : b + 1, :] * weight_ref[b : b + 1, :])
+            inv_col[lanes_of(b), :] = column(inv_ref[b : b + 1, :])
 
     for i in range(per_step):
         rate = rate_of(index_ref[step * per_step + i], slab)
         lanes = lanes_of(i)
-        products = head(c_ref, i).astype(F32) * (o_ref[:, lanes] * scale_col[...])
-        gain_out_ref[pl.ds(step * per_step + i, 1), :] = jnp.sum(products, axis=0, keepdims=True)
+        mixed_ref[0, :, lanes] = (o_ref[:, lanes] * inv_col[...] * gain_ref[:, lanes]).astype(BF16)
         k, v, g = head(k_ref, i), head(v_ref, i), g_ref[:, lanes]
         diagonal, below = decay_blocks(rate, False)
         carried = dot_nt(g, s_ref[i].astype(BF16)) * row_powers(rate, 1.0, 1.0, slab)
@@ -248,16 +261,8 @@
         qg_ref[0, b, lanes] = (dot_nn(lower, k) + carried[b]).astype(BF16)
 
 
-def key_value_kernel(
-    per_step, slab, index_ref, q_ref, k_ref, v_ref, g_ref, o_ref, inv_ref, gain_ref, mixed_ref, kl_ref, vl_ref, inv_col
-):
-    @pl.when(pl.program_id(0) == 0)
-    def _():
-        for b in range(slab // LANES):
-            inv_col[lanes_of(b), :] = column(inv_ref[b : b + 1, :])
-
+def key_value_kernel(per_step, slab, index_ref, q_ref, k_ref, v_ref, g_ref, kl_ref, vl_ref):
     for i in range(per_step):
-        mixed_ref[0, :, lanes_of(i)] = (o_ref[:, lanes_of(i)] * inv_col[...] * gain_ref[:, lanes_of(i)]).astype(BF16)
         rate = rate_of(index_ref[pl.program_id(0) * per_step + i], slab)
         lanes = lanes_of(i)
         q, k, v, g = head(q_ref, i), head(k_ref, i), head(v_ref, i), g_ref[:, lanes]
@@ -272,7 +277,8 @@
 
 
 def final_kernel(
-    heads, group, slab, size, index_hbm, r_ref, k_hbm, v_hbm, kl, vl, kg_hbm, vg_hbm, index, k, v, kg, vg, semaphores
+    heads, group, slab, size, index_hbm, r_ref, k_hbm, v_hbm, kl, vl, own_ref, other_ref, kg_hbm, vg_hbm, gain_hbm,
+    index, k, v, kg, vg, gain, semaphores,
 ):
     copies = Copies(semaphores)
     index_copy = copies.start(index_hbm, index)
@@ -280,9 +286,10 @@
     for first in range(0, heads, group):
         lanes = lanes_of(first, group)
         loads.append([copies.start(x.at[0, :, lanes], y.at[:, lanes]) for x, y in ((k_hbm, k), (v_hbm, v))])
+    gain[...] = own_ref[...] + other_ref[...]
     pieces = LANES // size
     index_copy.wait()
-    stores = []
+    stores = [copies.start(gain, gain_hbm)]
     for first in range(0, heads, group):
         wait_all(loads[first // group])
         for h in range(first, first + group):
@@ -343,11 +350,11 @@
 
     group = 2
     state_local = pl.pallas_call(
-        functools.partial(state_kernel, heads, group, slab),
+        functools.partial(state_kernel, heads, slab),
         in_specs=[anywhere] * 3,
         out_specs=anywhere,
         out_shape=state_out,
-        scratch_shapes=[index_held, held(BF16), held(BF16), state_held, semaphores(1 + 3 * heads // group)],
+        scratch_shapes=[index_held, held(BF16), held(BF16), state_held, semaphores(1 + 3 * heads)],
         compiler_params=params,
         name="state_local",
     )(decay_hbm, key, value)
@@ -366,21 +373,22 @@
     local_out = from_vmem(local_out)
 
     def scan(reverse, pieces, extra, name):
-        shape = (slabs, size + (heads if extra else 0), LANES)
+        shape = (slabs, size, LANES)
         return pl.pallas_call(
-            functools.partial(scan_kernel, slabs, slab, reverse, 4),
-            in_specs=[smem, smem, vmem] + [vmem] * len(extra),
-            out_specs=anywhere,
-            out_shape=pltpu.HBM(shape, F32),
+            functools.partial(scan_kernel, slabs, slab, size, reverse, 4),
+            in_specs=[smem, smem, vmem],
+            out_specs=[anywhere] + [vmem] * len(extra),
+            out_shape=[pltpu.HBM(shape, F32), *extra],
             scratch_shapes=[pltpu.VMEM(shape, F32), semaphores(slabs // 4)],
             compiler_params=params,
             name=name,
-        )(decay_index, place, pieces, *extra)
-
-    state_in = over_slabs(scan(False, sent, (), "prefix")).reshape(heads, LANES, LANES)
+        )(decay_index, place, pieces)
+
+    (before,) = scan(False, sent, [], "prefix")
+    state_in = over_slabs(before).reshape(heads, LANES, LANES)
 
     groups = lax.axis_size("head")
-    outputs, query_held, grad_n, stats = pl.pallas_call(
+    outputs, query_held, grad_y, stats = pl.pallas_call(
         functools.partial(output_kernel, heads, slab),
         in_specs=[anywhere, anywhere, vmem, vmem, anywhere, vmem, anywhere],
         out_specs=[vmem] * 4,
@@ -391,57 +399,59 @@
     )(decay_hbm, query, state_in, local_out, upstream, weight, gain_row)
     stats = lax.all_to_all(stats, "head", 0, 0, tiled=True)
 
+    return_shape = (slabs, size + heads, LANES)
     grad_out, outputs, return_local, inverse = pl.pallas_call(
-        functools.partial(grad_kernel, heads, group, slab, total_features),
-        in_specs=[anywhere, vmem, vmem, vmem, vmem],
+        functools.partial(grad_kernel, heads, group, slab, total_features, size),
+        in_specs=[anywhere, vmem, vmem, vmem, vmem, anywhere],
         out_specs=[anywhere, anywhere, anywhere, vmem],
-        out_shape=[pltpu.HBM((slab, features), BF16), token_f32, state_out, row_out],
+        out_shape=[pltpu.HBM((slab, features), BF16), token_f32, pltpu.HBM(return_shape, F32), row_out],
         scratch_shapes=[
-            index_held, held(BF16), state_held, columns, columns, semaphores(2 + 2 * heads // group)
+            index_held, gain_held, held(BF16), pltpu.VMEM(return_shape, F32), columns, columns,
+            semaphores(4 + 2 * heads // group),
         ],
         compiler_params=params,
         name="output_grad",
-    )(decay_hbm, stats, from_vmem(query_held), from_vmem(outputs), from_vmem(grad_n))
+    )(decay_hbm, stats, from_vmem(query_held), from_vmem(outputs), from_vmem(grad_y), gain_row)
     grad_out, outputs = from_hbm(grad_out), from_hbm(outputs)
-    returned = over_slabs(return_local.reshape(slabs, size, LANES))
-
-    query_grad, gain_part = pl.pallas_call(
+    returned = over_slabs(return_local)
+
+    mixed, query_grad = pl.pallas_call(
         functools.partial(query_grad_kernel, per_step, slab),
         grid=(steps,),
-        in_specs=[smem, token, token, flat, state, flat, token, token_row, token_row],
-        out_specs=[token, gain_out],
-        out_shape=[token_out, gain_f32],
+        in_specs=[smem, token, token, flat, state, flat, token_row, gain_spec],
+        out_specs=[token, token],
+        out_shape=[token_out, token_out],
         scratch_shapes=[columns],
         compiler_params=params,
         name="query_grads",
-    )(decay_index, key, value, grad_out, state_in, outputs, upstream, inverse, weight)
-    return_in = over_slabs(scan(True, returned, (gain_part,), "suffix"))
-
-    mixed, key_local, value_local = pl.pallas_call(
+    )(decay_index, key, value, grad_out, state_in, outputs, inverse, gain_row)
+    returned, mixed, query_grad = lax.optimization_barrier((returned, mixed, query_grad))
+    after, gain_sum = scan(True, returned, [gain_f32], "suffix")
+    return_in = over_slabs(after)
+
+    key_local, value_local = pl.pallas_call(
         functools.partial(key_value_kernel, per_step, slab),
         grid=(steps,),
-        in_specs=[smem, token, token, token, flat, flat, token_row, gain_spec],
-        out_specs=[token, flat, flat],
-        out_shape=[token_out, held(BF16), held(BF16)],
-        scratch_shapes=[columns],
+        in_specs=[smem, token, token, token, flat],
+        out_specs=[flat, flat],
+        out_shape=[held(BF16), held(BF16)],
         compiler_params=params,
         name="key_value_grads",
-    )(decay_index, query, key, value, grad_out, outputs, inverse, gain_row)
-
-    return_in, key_local, value_local = lax.optimization_barrier((return_in, key_local, value_local))
-    gain_sum = jnp.sum(return_in[:, size:], axis=0)
+    )(decay_index, query, key, value, grad_out)
+
+    gain_sum, key_local, value_local = lax.optimization_barrier((gain_sum, key_local, value_local))
     other_sum = lax.ppermute(gain_sum, "dp", [(i, 1 - i) for i in range(2)])
-    key_grad, value_grad = pl.pallas_call(
+    key_grad, value_grad, gain_grad = pl.pallas_call(
         functools.partial(final_kernel, heads, group, slab, size),
-        in_specs=[anywhere, vmem, anywhere, anywhere, vmem, vmem],
-        out_specs=[anywhere, anywhere],
-        out_shape=[token_out, token_out],
-        scratch_shapes=[index_held] + [held(BF16)] * 4 + [semaphores(1 + 4 * heads // group)],
+        in_specs=[anywhere, vmem, anywhere, anywhere, vmem, vmem, vmem, vmem],
+        out_specs=[anywhere] * 3,
+        out_shape=[token_out, token_out, pltpu.HBM((heads, LANES), F32)],
+        scratch_shapes=[index_held] + [held(BF16)] * 4
+        + [pltpu.VMEM((heads, LANES), F32), semaphores(2 + 4 * heads // group)],
         compiler_params=params,
         name="final_grads",
-    )(decay_hbm, return_in, key, value, from_vmem(key_local), from_vmem(value_local))
-    gain_grad = (gain_sum + other_sum).reshape(features)
-    return (mixed, query_grad, key_grad, value_grad, gain_grad)
+    )(decay_hbm, return_in, key, value, from_vmem(key_local), from_vmem(value_local), gain_sum, other_sum)
+    return (mixed, query_grad, key_grad, value_grad, gain_grad.reshape(features))
 
 
 def solution(mesh):

time: 95.6 us -> 92.5 us (0.968)
  the two profiles are of different devices: /device:TPU:1 before, /device:TPU:2 now
where the time goes in v3:
time: 92.5 us; the launch traced here: 91.6 us
  Pallas kernels  32.3 us (35%)
  starting transfers between devices  22.1 us (24%)
  waiting for transfers between devices  18.9 us (20%)
  blocking collectives  16.3 us (18%)
  between operations  2.04 us (2%)
    all_to_all x4, starting transfers between devices, over_slabs(): return lax.all_to_all(pieces, 'seq', 0, 0, tiled=True)  22 us
    all_to_all x4, waiting for transfers between devices, over_slabs(): return lax.all_to_all(pieces, 'seq', 0, 0, tiled=True)  17.7 us
    all_to_all x1, blocking collectives, on_device(): stats = lax.all_to_all(stats, 'head', 0, 0, tiled=True)  16.3 us
    pallas_call x1, Pallas kernels, on_device(): pl.pallas_call(functools.partial(query_grad_kernel, per_step, slab), grid...  6.12 us
    pallas_call x1, Pallas kernels, on_device(): pl.pallas_call(functools.partial(key_value_kernel, per_step, slab), grid=...  5.89 us
    pallas_call x1, Pallas kernels, on_device(): pl.pallas_call(functools.partial(local_kernel, per_step, slab, slab * sla...  5.2 us
    pallas_call x1, Pallas kernels, on_device(): pl.pallas_call(functools.partial(final_kernel, heads, group, slab, size),...  3.48 us
    pallas_call x1, Pallas kernels, on_device(): pl.pallas_call(functools.partial(grad_kernel, heads, group, slab, total_f...  3.21 us
  transfers between devices with their start and end apart: 5, of which 5 were waited for; matrix products, arithmetic and copies ran while one was open for 0% of the time, Pallas kernels for 19%

profile of v3, /device:TPU:2, one launch (start us, length us, event | category | flops | bytes accessed | tf_op | source)
XLA Modules:
  0.0 91.6 jit_solution(9664176113344811782)
XLA Ops:
  0.6 0.0 copy-start
  0.6 2.9 %state_local.1 = f32[8,128,128]{2,1,0:T(8,128)} custom-call(s32[8]{0:T(128)} %index_hbm.7, bf16[1,512,1024]{2,1,0:T(8,128)(2,1)} %k_hbm.3, bf16[1,512,1024]{2,1,0:T(8,128)(2,1)} %v_hbm.3), custom_call_target="tpu_custom_call" | custom-call | tf_op jit(solution)/shard_map/state_local/pallas_call | solution.py:352
  3.6 0.0 copy-start.2
  3.6 0.0 copy-start.3
  3.6 7.5 %all-to-all-start = ((f32[16,64,128]{2,1,0:T(8,128)}), f32[16,64,128]{2,1,0:T(8,128)S(1)}, u32[]{:S(2)}, u32[]{:S(2)}) async-start(f32[16,64,128]{2,1,0:T(8,128)} %bitcast.7), calls=%async_computation | async-start | bytes 1048576 | tf_op jit(solution)/shard_map/all_to_all | solution.py:349
  11.1 10.2 %all-to-all-done.x_ref = f32[16,64,128]{2,1,0:T(8,128)S(1)} async-done(((f32[16,64,128]{2,1,0:T(8,128)}), f32[16,64,128]{2,1,0:T(8,128)S(1)}, u32[]{:S(2)}, u32[]{:S(2)}) %all-to-all-start) | async-done | bytes 524320 | tf_op jit(solution)/shard_map/all_to_all | solution.py:349
  21.3 0.0 copy-done
  21.3 1.4 %prefix.1 = f32[16,64,128]{2,1,0:T(8,128)} custom-call(s32[8]{0:T(128)S(1)} %copy-done, s32[1]{0:T(128)} %bitcast.place_ref, f32[16,64,128]{2,1,0:T(8,128)S(1)} %all-to-all-done.x_ref), custom_call_target="tpu_custom_call" | custom-call | tf_op jit(solution)/shard_map/prefix/pallas_call | solution.py:377
  22.7 4.8 %all-to-all-start.1 = ((f32[16,64,128]{2,1,0:T(8,128)}), f32[16,64,128]{2,1,0:T(8,128)S(1)}, u32[]{:S(2)}, u32[]{:S(2)}) async-start(f32[16,64,128]{2,1,0:T(8,128)} %prefix.1), calls=%async_computation.1 | async-start | bytes 1048576 | tf_op jit(solution)/shard_map/all_to_all | solution.py:349
  28.8 0.0 copy-done.2
  28.8 0.0 copy-done.3
  28.8 5.2 %local_attention.1 = (f32[512,1024]{1,0:T(8,128)S(1)}, f32[4,128]{1,0:T(4,128)S(1)}) custom-call(s32[8]{0:T(128)S(1)} %copy-done, s32[1]{0:T(128)} %bitcast.place_ref, s32[1]{0:T(128)S(6)} %copy.16.length_ref, f32[1]{0:T(128)S(6)} %copy.15.advantage_ref, bf16[1,512,1024]{2,1,0:T(8,128)(2,1)} %q_ref.3, bf16[1,512,1024]{2,1,0:T(8,128)(2,1)} %k_hbm.3, ...), custom_call_target="tpu_custom_call" | custom-call | tf_op jit(solution)/shard_map/local_attention/pallas_call | solution.py:363
  34.0 2.8 %all-to-all-done.1 = f32[16,64,128]{2,1,0:T(8,128)S(1)} async-done(((f32[16,64,128]{2,1,0:T(8,128)}), f32[16,64,128]{2,1,0:T(8,128)S(1)}, u32[]{:S(2)}, u32[]{:S(2)}) %all-to-all-start.1) | async-done | bytes 524320 | tf_op jit(solution)/shard_map/all_to_all | solution.py:349
  36.8 2.7 %outputs.1 = (f32[512,1024]{1,0:T(8,128)S(1)}, bf16[512,1024]{1,0:T(8,128)(2,1)S(1)}, f32[512,1024]{1,0:T(8,128)S(1)}, f32[8,8,128]{2,1,0:T(8,128)S(1)}) custom-call(s32[8]{0:T(128)} %index_hbm.7, bf16[1,512,1024]{2,1,0:T(8,128)(2,1)} %q_ref.3, f32[8,128,128]{2,1,0:T(8,128)S(1)} %bitcast.5, f32[512,1024]{1,0:T(8,128)S(1)} %get-tuple-element.30.local, ...), custom_call_target="tpu_custom_call" | custom-call | tf_op jit(solution)/shard_map/outputs/pallas_call | solution.py:391
  39.4 16.3 %all_to_all.25.stat_ref = f32[8,8,128]{2,1,0:T(8,128)S(1)} all-to-all(f32[8,8,128]{2,1,0:T(8,128)S(1)} %get-tuple-element.32), channel_id=1, replica_groups=mesh['dp'=2,'seq'=16,'head'=8] {'head'}, dimensions={0} | all-to-all | bytes 65536 | tf_op jit(solution)/shard_map/all_to_all | solution.py:400
  55.7 0.0 copy-start.1
  55.7 3.2 %output_grad.1 = (bf16[512,1024]{1,0:T(8,128)(2,1)}, f32[512,1024]{1,0:T(8,128)}, f32[16,72,128]{2,1,0:T(8,128)}, f32[4,128]{1,0:T(4,128)S(1)}) custom-call(s32[8]{0:T(128)} %index_hbm.7, f32[8,8,128]{2,1,0:T(8,128)S(1)} %all_to_all.25.stat_ref, bf16[512,1024]{1,0:T(8,128)(2,1)S(1)} %get-tuple-element.33.q, f32[512,1024]{1,0:T(8,128)S(1)} %get-tuple-element.34.o, ...), custom_call_target="tpu_custom_call" | custom-call | tf_op jit(solution)/shard_map/output_grad/pallas_call | solution.py:403
  58.9 4.8 %all-to-all-start.3 = ((f32[16,72,128]{2,1,0:T(8,128)}), f32[16,72,128]{2,1,0:T(8,128)S(1)}, u32[]{:S(2)}, u32[]{:S(2)}) async-start(f32[16,72,128]{2,1,0:T(8,128)} %get-tuple-element.36), calls=%async_computation.3 | async-start | bytes 1179648 | tf_op jit(solution)/shard_map/all_to_all | solution.py:349
  63.8 0.0 copy-done.1
  63.8 6.1 %query_grads.1 = (bf16[1,512,1024]{2,1,0:T(8,128)(2,1)}, bf16[1,512,1024]{2,1,0:T(8,128)(2,1)}) custom-call(s32[8]{0:T(128)S(1)} %copy-done.1, bf16[1,512,1024]{2,1,0:T(8,128)(2,1)} %k_hbm.3, bf16[1,512,1024]{2,1,0:T(8,128)(2,1)} %v_hbm.3, bf16[512,1024]{1,0:T(8,128)(2,1)} %get-tuple-element.37.g_ref, f32[8,128,128]{2,1,0:T(8,128)S(1)} %bitcast.6, ...), custom_call_target="tpu_custom_call" | custom-call | tf_op jit(solution)/shard_map/query_grads/pallas_call | solution.py:418
  69.9 3.1 %all-to-all-done.3.x_ref = f32[16,72,128]{2,1,0:T(8,128)S(1)} async-done(((f32[16,72,128]{2,1,0:T(8,128)}), f32[16,72,128]{2,1,0:T(8,128)S(1)}, u32[]{:S(2)}, u32[]{:S(2)}) %all-to-all-start.3) | async-done | bytes 589856 | tf_op jit(solution)/shard_map/all_to_all | solution.py:349
  73.0 1.4 %suffix.1 = (f32[16,64,128]{2,1,0:T(8,128)}, f32[8,128]{1,0:T(8,128)S(1)}) custom-call(s32[8]{0:T(128)S(1)} %copy-done.1, s32[1]{0:T(128)} %bitcast.place_ref, f32[16,72,128]{2,1,0:T(8,128)S(1)} %all-to-all-done.3.x_ref), custom_call_target="tpu_custom_call" | custom-call | tf_op jit(solution)/shard_map/suffix/pallas_call | solution.py:377
  74.4 4.8 %all-to-all-start.4 = ((f32[16,64,128]{2,1,0:T(8,128)}), f32[16,64,128]{2,1,0:T(8,128)S(1)}, u32[]{:S(2)}, u32[]{:S(2)}) async-start(f32[16,64,128]{2,1,0:T(8,128)} %get-tuple-element.45), calls=%async_computation.4 | async-start | bytes 1048576 | tf_op jit(solution)/shard_map/all_to_all | solution.py:349
  79.2 5.9 %key_value_grads.1 = (bf16[512,1024]{1,0:T(8,128)(2,1)S(1)}, bf16[512,1024]{1,0:T(8,128)(2,1)S(1)}) custom-call(s32[8]{0:T(128)S(1)} %copy-done.1, bf16[1,512,1024]{2,1,0:T(8,128)(2,1)} %q_ref.3, bf16[1,512,1024]{2,1,0:T(8,128)(2,1)} %k_hbm.3, bf16[1,512,1024]{2,1,0:T(8,128)(2,1)} %v_hbm.3, bf16[512,1024]{1,0:T(8,128)(2,1)} %get-tuple-element.37.g_ref), custom_call_target="tpu_custom_call" | custom-call | tf_op jit(solution)/shard_map/key_value_grads/pallas_call | solution.py:432
  85.1 0.1 collective-permute-start
  85.2 1.2 %collective-permute-done.other_ref = f32[8,128]{1,0:T(8,128)S(1)} collective-permute-done((f32[8,128]{1,0:T(8,128)S(1)}, f32[8,128]{1,0:T(8,128)S(1)}, u32[]{:S(2)}, u32[]{:S(2)}) %collective-permute-start) | collective-permute-done | bytes 4128 | tf_op jit(solution)/shard_map/ppermute | solution.py:443
  86.4 1.7 %all-to-all-done.4.r_ref = f32[16,64,128]{2,1,0:T(8,128)S(1)} async-done(((f32[16,64,128]{2,1,0:T(8,128)}), f32[16,64,128]{2,1,0:T(8,128)S(1)}, u32[]{:S(2)}, u32[]{:S(2)}) %all-to-all-start.4) | async-done | bytes 524320 | tf_op jit(solution)/shard_map/all_to_all | solution.py:349
  88.1 3.5 %final_grads.1 = (bf16[1,512,1024]{2,1,0:T(8,128)(2,1)}, bf16[1,512,1024]{2,1,0:T(8,128)(2,1)}, f32[8,128]{1,0:T(8,128)}) custom-call(s32[8]{0:T(128)} %index_hbm.7, f32[16,64,128]{2,1,0:T(8,128)S(1)} %all-to-all-done.4.r_ref, bf16[1,512,1024]{2,1,0:T(8,128)(2,1)} %k_hbm.3, bf16[1,512,1024]{2,1,0:T(8,128)(2,1)} %v_hbm.3, ...), custom_call_target="tpu_custom_call" | custom-call | tf_op jit(solution)/shard_map/final_grads/pallas_call | solution.py:444
Async XLA Ops:
  0.6 20.6 %copy-start = (s32[8]{0:T(128)S(1)}, s32[8]{0:T(128)}, u32[]{:S(2)}) copy-start(s32[8]{0:T(128)} %index_hbm.7) | copy-start | bytes 100
  3.6 25.2 %copy-start.2 = (s32[1,512]{1,0:T(1,128)S(1)}, s32[1,512]{1,0:T(1,128)}, u32[]{:S(2)}) copy-start(s32[1,512]{1,0:T(1,128)} %mask_ref.1) | copy-start | bytes 6148
  3.6 25.2 %copy-start.3 = (f32[1,512]{1,0:T(1,128)S(1)}, f32[1,512]{1,0:T(1,128)}, u32[]{:S(2)}) copy-start(f32[1,512]{1,0:T(1,128)} %imp_ref.1) | copy-start | bytes 6148
  3.6 17.7 %all-to-all-start = ((f32[16,64,128]{2,1,0:T(8,128)}), f32[16,64,128]{2,1,0:T(8,128)S(1)}, u32[]{:S(2)}, u32[]{:S(2)}) async-start(f32[16,64,128]{2,1,0:T(8,128)} %bitcast.7), calls=%async_computation | async-start | bytes 1048576 | tf_op jit(solution)/shard_map/all_to_all | solution.py:349
  22.7 14.1 %all-to-all-start.1 = ((f32[16,64,128]{2,1,0:T(8,128)}), f32[16,64,128]{2,1,0:T(8,128)S(1)}, u32[]{:S(2)}, u32[]{:S(2)}) async-start(f32[16,64,128]{2,1,0:T(8,128)} %prefix.1), calls=%async_computation.1 | async-start | bytes 1048576 | tf_op jit(solution)/shard_map/all_to_all | solution.py:349
  55.7 8.1 %copy-start.1 = (s32[8]{0:T(128)S(1)}, s32[8]{0:T(128)}, u32[]{:S(2)}) copy-start(s32[8]{0:T(128)} %index_hbm.7) | copy-start | bytes 100
  58.9 14.1 %all-to-all-start.3 = ((f32[16,72,128]{2,1,0:T(8,128)}), f32[16,72,128]{2,1,0:T(8,128)S(1)}, u32[]{:S(2)}, u32[]{:S(2)}) async-start(f32[16,72,128]{2,1,0:T(8,128)} %get-tuple-element.36), calls=%async_computation.3 | async-start | bytes 1179648 | tf_op jit(solution)/shard_map/all_to_all | solution.py:349
  74.4 13.7 %all-to-all-start.4 = ((f32[16,64,128]{2,1,0:T(8,128)}), f32[16,64,128]{2,1,0:T(8,128)S(1)}, u32[]{:S(2)}, u32[]{:S(2)}) async-start(f32[16,64,128]{2,1,0:T(8,128)} %get-tuple-element.45), calls=%async_computation.4 | async-start | bytes 1048576 | tf_op jit(solution)/shard_map/all_to_all | solution.py:349
  85.1 1.3 %collective-permute-start = (f32[8,128]{1,0:T(8,128)S(1)}, f32[8,128]{1,0:T(8,128)S(1)}, u32[]{:S(2)}, u32[]{:S(2)}) collective-permute-start(f32[8,128]{1,0:T(8,128)S(1)} %get-tuple-element.51.own_ref), channel_id=1, source_target_pairs={{0,128},{128,0},{1,129},{129,1},{2,130},{130,2},{3,131},{131,3},{4... | collective-permute-start | bytes 12296 | tf_op jit(solution)/shard_map/ppermute | solution.py:443

commit v4 on v3

--- a/solution.py
+++ b/solution.py
@@ -84,17 +84,19 @@
     return jnp.broadcast_to(row, (LANES, LANES)).T
 
 
-def state_kernel(heads, slab, index_hbm, k_hbm, v_hbm, out_hbm, index, k, v, out, semaphores):
+def state_kernel(heads, slab, index_hbm, k_hbm, v_hbm, out_hbm, rates, index, k, v, out, semaphores):
     copies = Copies(semaphores)
     index_copy = copies.start(index_hbm, index)
     spans = [slice(at, at + HALF) for at in range(0, slab, HALF)]
     loads = [[copies.start(x.at[0, rows], y.at[rows]) for x, y in ((k_hbm, k), (v_hbm, v))] for rows in spans]
     stores = []
     index_copy.wait()
+    for h in range(heads):
+        rates[h : h + 1, :] = rate_of(index[h], slab)
     for rows, load in zip(spans, loads):
         wait_all(load)
         for h in range(heads):
-            powers = row_powers(rate_of(index[h], slab), slab - 1.0 - rows.start, -1.0, HALF)
+            powers = row_powers(rates[h : h + 1, :], slab - 1.0 - rows.start, -1.0, HALF)
             decayed = (k[rows, lanes_of(h)].astype(F32) * powers).astype(BF16)
             term = dot_tn(decayed, v[rows, lanes_of(h)])
             out[h] = term if rows.start == 0 else out[h] + term
@@ -104,10 +106,10 @@
     wait_all(stores)
 
 
-def scan_kernel(slabs, slab, size, reverse, group, index_ref, place_ref, x_ref, out_hbm, *refs):
+def scan_kernel(slabs, slab, size, reverse, group, place_ref, rates_ref, x_ref, out_hbm, *refs):
     extra, (out, semaphores) = refs[:-2], refs[-2:]
     copies = Copies(semaphores)
-    rate = rate_of(index_ref[(place_ref[0] * size) // LANES], slab)
+    rate = rates_ref[pl.ds((place_ref[0] * size) // LANES, 1), :]
     factor = jnp.exp2(-rate * float(slab))
     running = jnp.zeros((size, LANES), F32)
     order = list(reversed(range(slabs))) if reverse else list(range(slabs))
@@ -127,21 +129,23 @@
 
 
 def local_kernel(
-    per_step, slab, total, index_ref, place_ref, length_ref, advantage_ref, q_ref, k_ref, v_ref, mask_ref, imp_ref,
-    out_ref, weight_ref,
+    per_step, slab, total, place_ref, length_ref, advantage_ref, rates_ref, q_ref, k_ref, v_ref, c_ref, mask_ref, imp_ref,
+    out_ref, weight_ref, q_first_ref, c_first_ref,
 ):
     @pl.when(pl.program_id(0) == 0)
     def _():
         at = place_ref[0] * slab + lax.broadcasted_iota(jnp.int32, (1, slab), 1)
-        inside = (at < length_ref[0]).astype(F32)
-        length = jnp.full((1, slab), length_ref[0].astype(F32), F32)
+        length = length_ref[...]
+        inside = (at < length).astype(F32)
         weight = mask_ref[...].astype(F32) * inside * jnp.minimum(imp_ref[...], clip_high)
-        weight = weight * advantage_ref[0] * (float(total) / length)
+        weight = weight * advantage_ref[...] * (float(total) / length.astype(F32))
         for b in range(slab // LANES):
             weight_ref[b : b + 1, :] = weight[:, lanes_of(b)]
 
+    q_first_ref[...] = q_ref[0, :LANES, :]
+    c_first_ref[...] = c_ref[0]
     for i in range(per_step):
-        rate = rate_of(index_ref[pl.program_id(0) * per_step + i], slab)
+        rate = rates_ref[pl.ds(pl.program_id(0) * per_step + i, 1), :]
         diagonal, below = decay_blocks(rate, False)
         q, k, v = head(q_ref, i), head(k_ref, i), head(v_ref, i)
         lanes = lanes_of(i)
@@ -153,40 +157,36 @@
 
 
 def output_kernel(
-    heads, slab, index_hbm, q_hbm, s_ref, local, c_hbm, weight_ref, gain_hbm, out, q, grad_y, stat_ref,
-    index, gain, c, s, semaphores,
+    heads, slab, rates, q_hbm, s_ref, local, c_hbm, weight_ref, gain, q_first, c_first, out, q, grad_y, stat_ref,
+    c, s, semaphores,
 ):
     copies = Copies(semaphores)
-    small = [copies.start(index_hbm, index), copies.start(gain_hbm, gain)]
-    loads = []
-    span = HALF // LANES
-    for b in range(0, slab // LANES, span):
-        rows = lanes_of(b, span)
-        loads.append([
-            copies.start(q_hbm.at[0, rows], q.at[rows]),
-            copies.start(c_hbm.at[0, rows], c.at[rows]),
-        ])
+    spans = [(0, 1), (1, 1), (2, slab // LANES - 2)]
+    loads = [[]]
+    for first, count in spans[1:]:
+        rows = lanes_of(first, count)
+        loads.append([copies.start(q_hbm.at[0, rows], q.at[rows]), copies.start(c_hbm.at[0, rows], c.at[rows])])
+    q[:LANES] = q_first[...]
+    c[:LANES] = c_first[...]
     for h in range(heads):
         s[h] = s_ref[h].astype(BF16)
-    wait_all(small)
     square_rows, cross_rows = [], []
-    for b in range(0, slab // LANES, span):
-        rows = lanes_of(b, span)
-        weight = jnp.concatenate([column(weight_ref[x : x + 1, :]) for x in range(b, b + span)], axis=0)
-        squares = jnp.zeros((HALF, LANES), F32)
-        crosses = jnp.zeros((HALF, LANES), F32)
-        wait_all(loads[b // span])
+    for (first, count), load in zip(spans, loads):
+        rows = lanes_of(first, count)
+        weight = jnp.concatenate([column(weight_ref[x : x + 1, :]) for x in range(first, first + count)], axis=0)
+        squares = jnp.zeros((count * LANES, LANES), F32)
+        crosses = jnp.zeros((count * LANES, LANES), F32)
+        wait_all(load)
         for h in range(heads):
-            rate = rate_of(index[h], slab)
             lanes = lanes_of(h)
             carried = dot_nn(q[rows, lanes], s[h])
-            o = local[rows, lanes] + carried * row_powers(rate, b * LANES + 1.0, 1.0, HALF)
+            o = local[rows, lanes] + carried * row_powers(rates[h : h + 1, :], first * LANES + 1.0, 1.0, count * LANES)
             out[rows, lanes] = o
             squares += o * o
             grad = c[rows, lanes].astype(F32) * weight
             grad_y[rows, lanes] = grad
             crosses += (grad * gain[:, lanes]) * o
-        for x in range(span):
+        for x in range(count):
             square_rows.append(jnp.sum(squares[lanes_of(x)].T, axis=0, keepdims=True))
             cross_rows.append(jnp.sum(crosses[lanes_of(x)].T, axis=0, keepdims=True))
     stats = jnp.concatenate(square_rows + cross_rows, axis=0)
@@ -195,11 +195,10 @@
 
 
 def grad_kernel(
-    heads, group, slab, features, size, index_hbm, stat_ref, q, o, grad_y, gain_hbm,
-    g_hbm, o_hbm, ret_hbm, inv_ref, index, gain, g, ret, inv_col, mean_col, semaphores,
+    heads, group, slab, features, size, rates, stat_ref, q, o, grad_y, gain,
+    g_hbm, o_hbm, ret_hbm, inv_ref, g, ret, inv_col, mean_col, semaphores,
 ):
     copies = Copies(semaphores)
-    small = [copies.start(index_hbm, index), copies.start(gain_hbm, gain)]
     stores = [copies.start(o, o_hbm)]
     stats = jnp.sum(stat_ref[...], axis=0)
     blocks = slab // LANES
@@ -210,12 +209,11 @@
         rows = lanes_of(b)
         inv_col[rows, :] = column(inverse[b : b + 1])
         mean_col[rows, :] = column(mean[b : b + 1])
-    wait_all(small)
     pieces = LANES // size
     gain_rows = []
     for first in range(0, heads, group):
         for h in range(first, first + group):
-            rate = rate_of(index[h], slab)
+            rate = rates[h : h + 1, :]
             lanes = lanes_of(h)
             normed = o[:, lanes] * inv_col[...]
             gain_rows.append(jnp.sum(grad_y[:, lanes] * normed, axis=0, keepdims=True))
@@ -238,7 +236,7 @@
 
 
 def query_grad_kernel(
-    per_step, slab, index_ref, k_ref, v_ref, g_ref, s_ref, o_ref, inv_ref, gain_ref, mixed_ref, qg_ref, inv_col
+    per_step, slab, rates_ref, k_ref, v_ref, g_ref, s_ref, o_ref, inv_ref, gain_ref, mixed_ref, qg_ref, inv_col
 ):
     step = pl.program_id(0)
 
@@ -248,7 +246,7 @@
             inv_col[lanes_of(b), :] = column(inv_ref[b : b + 1, :])
 
     for i in range(per_step):
-        rate = rate_of(index_ref[step * per_step + i], slab)
+        rate = rates_ref[pl.ds(step * per_step + i, 1), :]
         lanes = lanes_of(i)
         mixed_ref[0, :, lanes] = (o_ref[:, lanes] * inv_col[...] * gain_ref[:, lanes]).astype(BF16)
         k, v, g = head(k_ref, i), head(v_ref, i), g_ref[:, lanes]
@@ -261,9 +259,16 @@
         qg_ref[0, b, lanes] = (dot_nn(lower, k) + carried[b]).astype(BF16)
 
 
-def key_value_kernel(per_step, slab, index_ref, q_ref, k_ref, v_ref, g_ref, kl_ref, vl_ref):
+def key_value_kernel(
+    per_step, slab, rates_ref, q_ref, k_ref, v_ref, g_ref, kl_ref, vl_ref, k_first_ref, v_first_ref
+):
+    @pl.when(pl.program_id(0) == 0)
+    def _():
+        k_first_ref[...] = k_ref[0]
+        v_first_ref[...] = v_ref[0]
+
     for i in range(per_step):
-        rate = rate_of(index_ref[pl.program_id(0) * per_step + i], slab)
+        rate = rates_ref[pl.ds(pl.program_id(0) * per_step + i, 1), :]
         lanes = lanes_of(i)
         q, k, v, g = head(q_ref, i), head(k_ref, i), head(v_ref, i), g_ref[:, lanes]
         diagonal, below = decay_blocks(rate, True)
@@ -277,27 +282,26 @@
 
 
 def final_kernel(
-    heads, group, slab, size, index_hbm, r_ref, k_hbm, v_hbm, kl, vl, own_ref, other_ref, kg_hbm, vg_hbm, gain_hbm,
-    index, k, v, kg, vg, gain, semaphores,
+    heads, group, slab, size, rates, r_ref, k_hbm, v_hbm, kl, vl, k_first, v_first, own_ref, other_ref,
+    kg_hbm, vg_hbm, gain_hbm, k, v, kg, vg, gain, semaphores,
 ):
     copies = Copies(semaphores)
-    index_copy = copies.start(index_hbm, index)
-    loads = []
-    for first in range(0, heads, group):
+    loads = [[]]
+    for first in range(group, heads, group):
         lanes = lanes_of(first, group)
         loads.append([copies.start(x.at[0, :, lanes], y.at[:, lanes]) for x, y in ((k_hbm, k), (v_hbm, v))])
     gain[...] = own_ref[...] + other_ref[...]
     pieces = LANES // size
-    index_copy.wait()
     stores = [copies.start(gain, gain_hbm)]
     for first in range(0, heads, group):
         wait_all(loads[first // group])
+        source = (k_first, v_first) if first == 0 else (k, v)
         for h in range(first, first + group):
             lanes = lanes_of(h)
-            to_next = row_powers(rate_of(index[h], slab), float(slab), -1.0, slab)
+            to_next = row_powers(rates[h : h + 1, :], float(slab), -1.0, slab)
             back = jnp.concatenate([r_ref[h * pieces + p, :size] for p in range(pieces)], axis=0).astype(BF16)
-            kg[:, lanes] = (kl[:, lanes].astype(F32) + dot_nt(v[:, lanes], back) * to_next).astype(BF16)
-            vg[:, lanes] = (vl[:, lanes].astype(F32) + dot_nn(k[:, lanes], back) * to_next).astype(BF16)
+            kg[:, lanes] = (kl[:, lanes].astype(F32) + dot_nt(source[1][:, lanes], back) * to_next).astype(BF16)
+            vg[:, lanes] = (vl[:, lanes].astype(F32) + dot_nn(source[0][:, lanes], back) * to_next).astype(BF16)
         lanes = lanes_of(first, group)
         stores += [copies.start(x.at[:, lanes], y.at[0, :, lanes]) for x, y in ((kg, kg_hbm), (vg, vg_hbm))]
     wait_all(stores)
@@ -314,7 +318,7 @@
     steps = heads // per_step
     wide = per_step * LANES
     blocks = slab // LANES
-    gain_row = from_hbm(norm_gain.reshape(1, features))
+    gain_row = norm_gain.reshape(1, features)
     decay_hbm, query, key, value, upstream = map(from_hbm, (decay_index, query_rows, key_rows, value_rows, cotangent))
 
     smem = pl.BlockSpec(memory_space=pltpu.SMEM)
@@ -326,6 +330,7 @@
     state = pl.BlockSpec((per_step, LANES, LANES), lambda i: (i, 0, 0))
     token_row = pl.BlockSpec((blocks, LANES), lambda i: (0, 0))
     gain_out = pl.BlockSpec((heads, LANES), lambda i: (0, 0))
+    one = pl.BlockSpec((1, slab), lambda i: (0, 0))
     token_f32 = pltpu.HBM((slab, features), F32)
     token_out = pltpu.HBM(query_rows.shape, BF16)
     state_out = pltpu.HBM((heads, LANES, LANES), F32)
@@ -340,7 +345,6 @@
         return pltpu.SemaphoreType.DMA((count,))
 
     index_held = pltpu.SMEM((heads,), jnp.int32)
-    gain_held = pltpu.VMEM((1, features), F32)
     state_held = pltpu.VMEM((heads, LANES, LANES), F32)
     state_half = pltpu.VMEM((heads, LANES, LANES), BF16)
     columns = pltpu.VMEM((slab, LANES), F32)
@@ -349,40 +353,46 @@
         return lax.all_to_all(pieces, "seq", 0, 0, tiled=True)
 
     group = 2
-    state_local = pl.pallas_call(
+    state_local, rates = pl.pallas_call(
         functools.partial(state_kernel, heads, slab),
         in_specs=[anywhere] * 3,
-        out_specs=anywhere,
-        out_shape=state_out,
+        out_specs=[anywhere, vmem],
+        out_shape=[state_out, gain_f32],
         scratch_shapes=[index_held, held(BF16), held(BF16), state_held, semaphores(1 + 3 * heads)],
         compiler_params=params,
         name="state_local",
     )(decay_hbm, key, value)
     sent = over_slabs(state_local.reshape(slabs, size, LANES))
-
-    local_out, weight = pl.pallas_call(
+    length_row = jnp.broadcast_to(lengths.reshape(1, 1), (1, slab))
+    advantage_row = jnp.broadcast_to(advantage.reshape(1, 1), (1, slab))
+    sent, length_row, advantage_row = lax.optimization_barrier((sent, length_row, advantage_row))
+
+    first_rows = pltpu.VMEM((LANES, features), BF16)
+    local_out, weight, query_first, upstream_first = pl.pallas_call(
         functools.partial(local_kernel, per_step, slab, slab * slabs),
         grid=(steps,),
-        in_specs=[smem, smem, smem, smem, token, token, token]
+        in_specs=[smem, one, one, gain_out, token, token, token, pl.BlockSpec((1, LANES, wide), lambda i: (0, 0, i))]
         + [pl.BlockSpec((1, slab), lambda i: (0, 0))] * 2,
-        out_specs=[flat, token_row],
-        out_shape=[pltpu.VMEM((slab, features), F32), row_out],
+        out_specs=[flat, token_row] + [pl.BlockSpec((LANES, wide), lambda i: (0, i))] * 2,
+        out_shape=[held(F32), row_out, first_rows, first_rows],
         compiler_params=params,
         name="local_attention",
-    )(decay_index, place, lengths, advantage, query, key, value, loss_mask, importance)
+    )(
+        place, length_row, advantage_row, rates, query, key, value, upstream, loss_mask, importance
+    )
     local_out = from_vmem(local_out)
 
     def scan(reverse, pieces, extra, name):
         shape = (slabs, size, LANES)
         return pl.pallas_call(
             functools.partial(scan_kernel, slabs, slab, size, reverse, 4),
-            in_specs=[smem, smem, vmem],
+            in_specs=[smem, vmem, vmem],
             out_specs=[anywhere] + [vmem] * len(extra),
             out_shape=[pltpu.HBM(shape, F32), *extra],
             scratch_shapes=[pltpu.VMEM(shape, F32), semaphores(slabs // 4)],
             compiler_params=params,
             name=name,
-        )(decay_index, place, pieces)
+        )(place, rates, pieces)
 
     (before,) = scan(False, sent, [], "prefix")
     state_in = over_slabs(before).reshape(heads, LANES, LANES)
@@ -390,67 +400,71 @@
     groups = lax.axis_size("head")
     outputs, query_held, grad_y, stats = pl.pallas_call(
         functools.partial(output_kernel, heads, slab),
-        in_specs=[anywhere, anywhere, vmem, vmem, anywhere, vmem, anywhere],
+        in_specs=[vmem, anywhere, vmem, vmem, anywhere, vmem, vmem, vmem, vmem],
         out_specs=[vmem] * 4,
         out_shape=[held(F32), held(BF16), held(F32), jax.ShapeDtypeStruct((groups, 2 * blocks, LANES), F32)],
-        scratch_shapes=[index_held, gain_held, held(BF16), state_half, semaphores(2 + 2 * blocks)],
+        scratch_shapes=[held(BF16), state_half, semaphores(4)],
         compiler_params=params,
         name="outputs",
-    )(decay_hbm, query, state_in, local_out, upstream, weight, gain_row)
+    )(
+        rates, query, state_in, local_out, upstream, weight, gain_row, from_vmem(query_first), from_vmem(upstream_first)
+    )
     stats = lax.all_to_all(stats, "head", 0, 0, tiled=True)
 
     return_shape = (slabs, size + heads, LANES)
     grad_out, outputs, return_local, inverse = pl.pallas_call(
         functools.partial(grad_kernel, heads, group, slab, total_features, size),
-        in_specs=[anywhere, vmem, vmem, vmem, vmem, anywhere],
+        in_specs=[vmem] * 6,
         out_specs=[anywhere, anywhere, anywhere, vmem],
         out_shape=[pltpu.HBM((slab, features), BF16), token_f32, pltpu.HBM(return_shape, F32), row_out],
         scratch_shapes=[
-            index_held, gain_held, held(BF16), pltpu.VMEM(return_shape, F32), columns, columns,
-            semaphores(4 + 2 * heads // group),
+            held(BF16), pltpu.VMEM(return_shape, F32), columns, columns, semaphores(2 + 2 * heads // group)
         ],
         compiler_params=params,
         name="output_grad",
-    )(decay_hbm, stats, from_vmem(query_held), from_vmem(outputs), from_vmem(grad_y), gain_row)
+    )(rates, stats, from_vmem(query_held), from_vmem(outputs), from_vmem(grad_y), gain_row)
     grad_out, outputs = from_hbm(grad_out), from_hbm(outputs)
     returned = over_slabs(return_local)
 
     mixed, query_grad = pl.pallas_call(
         functools.partial(query_grad_kernel, per_step, slab),
         grid=(steps,),
-        in_specs=[smem, token, token, flat, state, flat, token_row, gain_spec],
+        in_specs=[gain_out, token, token, flat, state, flat, token_row, gain_spec],
         out_specs=[token, token],
         out_shape=[token_out, token_out],
         scratch_shapes=[columns],
         compiler_params=params,
         name="query_grads",
-    )(decay_index, key, value, grad_out, state_in, outputs, inverse, gain_row)
+    )(rates, key, value, grad_out, state_in, outputs, inverse, gain_row)
     returned, mixed, query_grad = lax.optimization_barrier((returned, mixed, query_grad))
     after, gain_sum = scan(True, returned, [gain_f32], "suffix")
     return_in = over_slabs(after)
 
-    key_local, value_local = pl.pallas_call(
+    first_heads = pltpu.VMEM((slab, wide), BF16)
+    key_local, value_local, key_first, value_first = pl.pallas_call(
         functools.partial(key_value_kernel, per_step, slab),
         grid=(steps,),
-        in_specs=[smem, token, token, token, flat],
-        out_specs=[flat, flat],
-        out_shape=[held(BF16), held(BF16)],
+        in_specs=[gain_out, token, token, token, flat],
+        out_specs=[flat, flat] + [pl.BlockSpec((slab, wide), lambda i: (0, 0))] * 2,
+        out_shape=[held(BF16), held(BF16), first_heads, first_heads],
         compiler_params=params,
         name="key_value_grads",
-    )(decay_index, query, key, value, grad_out)
+    )(rates, query, key, value, grad_out)
 
     gain_sum, key_local, value_local = lax.optimization_barrier((gain_sum, key_local, value_local))
     other_sum = lax.ppermute(gain_sum, "dp", [(i, 1 - i) for i in range(2)])
     key_grad, value_grad, gain_grad = pl.pallas_call(
-        functools.partial(final_kernel, heads, group, slab, size),
-        in_specs=[anywhere, vmem, anywhere, anywhere, vmem, vmem, vmem, vmem],
+        functools.partial(final_kernel, heads, per_step, slab, size),
+        in_specs=[vmem, vmem, anywhere, anywhere] + [vmem] * 6,
         out_specs=[anywhere] * 3,
         out_shape=[token_out, token_out, pltpu.HBM((heads, LANES), F32)],
-        scratch_shapes=[index_held] + [held(BF16)] * 4
-        + [pltpu.VMEM((heads, LANES), F32), semaphores(2 + 4 * heads // group)],
+        scratch_shapes=[held(BF16)] * 4 + [pltpu.VMEM((heads, LANES), F32), semaphores(1 + 4 * steps)],
         compiler_params=params,
         name="final_grads",
-    )(decay_hbm, return_in, key, value, from_vmem(key_local), from_vmem(value_local), gain_sum, other_sum)
+    )(
+        rates, return_in, key, value, from_vmem(key_local), from_vmem(value_local), from_vmem(key_first),
+        from_vmem(value_first), gain_sum, other_sum,
+    )
     return (mixed, query_grad, key_grad, value_grad, gain_grad.reshape(features))
 
 

time: 92.5 us -> 90 us (0.973)
  Pallas kernels: 32.3 us -> 29.9 us
    pallas_call x2, Pallas kernels: 2.79 us -> 1.68 us  [scan(): pl.pallas_call(functools.partial(scan_kernel, slabs, slab, size, reverse,...]
where the time goes in v4:
time: 90 us; the launch traced here: 89.1 us
  Pallas kernels  29.9 us (33%)
  starting transfers between devices  22.1 us (25%)
  waiting for transfers between devices  18.8 us (21%)
  blocking collectives  16.3 us (18%)
  between operations  2.03 us (2%)
    all_to_all x4, starting transfers between devices, over_slabs(): return lax.all_to_all(pieces, 'seq', 0, 0, tiled=True)  22 us
    all_to_all x4, waiting for transfers between devices, over_slabs(): return lax.all_to_all(pieces, 'seq', 0, 0, tiled=True)  17.7 us
    all_to_all x1, blocking collectives, on_device(): stats = lax.all_to_all(stats, 'head', 0, 0, tiled=True)  16.3 us
    pallas_call x1, Pallas kernels, on_device(): pl.pallas_call(functools.partial(query_grad_kernel, per_step, slab), grid...  6.1 us
    pallas_call x1, Pallas kernels, on_device(): pl.pallas_call(functools.partial(key_value_kernel, per_step, slab), grid=...  5.89 us
    pallas_call x1, Pallas kernels, on_device(): pl.pallas_call(functools.partial(local_kernel, per_step, slab, slab * sla...  5.28 us
    pallas_call x1, Pallas kernels, on_device(): pl.pallas_call(functools.partial(final_kernel, heads, per_step, slab, siz...  3.28 us
    pallas_call x1, Pallas kernels, on_device(): pl.pallas_call(functools.partial(state_kernel, heads, slab), in_specs=[an...  2.92 us
  transfers between devices with their start and end apart: 5, of which 5 were waited for; matrix products, arithmetic and copies ran while one was open for 0% of the time, Pallas kernels for 19%

profile of v4, /device:TPU:2, one launch (start us, length us, event | category | flops | bytes accessed | tf_op | source)
XLA Modules:
  0.0 89.1 jit_solution(16073984931070480442)
XLA Ops:
  0.6 2.9 %state_local.1 = (f32[8,128,128]{2,1,0:T(8,128)}, f32[8,128]{1,0:T(8,128)S(1)}) custom-call(s32[8]{0:T(128)} %index_hbm.1, bf16[1,512,1024]{2,1,0:T(8,128)(2,1)} %k_hbm.3, bf16[1,512,1024]{2,1,0:T(8,128)(2,1)} %v_hbm.3), custom_call_target="tpu_custom_call" | custom-call | tf_op jit(solution)/shard_map/state_local/pallas_call | solution.py:356
  3.6 0.0 copy-start.1
  3.6 0.0 copy-start.2
  3.6 7.5 %all-to-all-start = ((f32[16,64,128]{2,1,0:T(8,128)}), f32[16,64,128]{2,1,0:T(8,128)S(1)}, u32[]{:S(2)}, u32[]{:S(2)}) async-start(f32[16,64,128]{2,1,0:T(8,128)} %bitcast.14), calls=%async_computation | async-start | bytes 1048576 | tf_op jit(solution)/shard_map/all_to_all | solution.py:353
  12.4 8.9 %all-to-all-done.x_ref = f32[16,64,128]{2,1,0:T(8,128)S(1)} async-done(((f32[16,64,128]{2,1,0:T(8,128)}), f32[16,64,128]{2,1,0:T(8,128)S(1)}, u32[]{:S(2)}, u32[]{:S(2)}) %all-to-all-start) | async-done | bytes 524320 | tf_op jit(solution)/shard_map/all_to_all | solution.py:353
  21.2 0.8 prefix.1
  22.1 4.8 %all-to-all-start.1 = ((f32[16,64,128]{2,1,0:T(8,128)}), f32[16,64,128]{2,1,0:T(8,128)S(1)}, u32[]{:S(2)}, u32[]{:S(2)}) async-start(f32[16,64,128]{2,1,0:T(8,128)} %prefix.1), calls=%async_computation.1 | async-start | bytes 1048576 | tf_op jit(solution)/shard_map/all_to_all | solution.py:353
  26.9 0.0 copy-done.1
  26.9 0.0 copy-done.2
  26.9 0.0 copy-start
  27.0 5.3 %local_attention.1 = (f32[512,1024]{1,0:T(8,128)S(1)}, f32[4,128]{1,0:T(4,128)S(1)}, bf16[128,1024]{1,0:T(8,128)(2,1)S(1)}, bf16[128,1024]{1,0:T(8,128)(2,1)S(1)}) custom-call(s32[1]{0:T(128)} %bitcast.place_ref, s32[1,512]{1,0:T(1,128)S(1)} %broadcast_in_dim.15.length_ref, f32[1,512]{1,0:T(1,128)S(1)} %broadcast_in_dim.17.advantage_ref, ...), custom_call_target="tpu_custom_call" | custom-call | tf_op jit(solution)/shard_map/local_attention/pallas_call | solution.py:371
  32.2 4.0 %all-to-all-done.1 = f32[16,64,128]{2,1,0:T(8,128)S(1)} async-done(((f32[16,64,128]{2,1,0:T(8,128)}), f32[16,64,128]{2,1,0:T(8,128)S(1)}, u32[]{:S(2)}, u32[]{:S(2)}) %all-to-all-start.1) | async-done | bytes 524320 | tf_op jit(solution)/shard_map/all_to_all | solution.py:353
  36.2 0.0 copy-done
  36.2 2.2 %outputs.1 = (f32[512,1024]{1,0:T(8,128)S(1)}, bf16[512,1024]{1,0:T(8,128)(2,1)S(1)}, f32[512,1024]{1,0:T(8,128)S(1)}, f32[8,8,128]{2,1,0:T(8,128)S(1)}) custom-call(f32[8,128]{1,0:T(8,128)S(1)} %get-tuple-element.39.rates_ref.rates, bf16[1,512,1024]{2,1,0:T(8,128)(2,1)} %q_ref.3, f32[8,128,128]{2,1,0:T(8,128)S(1)} %bitcast.9, ...), custom_call_target="tpu_custom_call" | custom-call | tf_op jit(solution)/shard_map/outputs/pallas_call | solution.py:401
  38.4 16.3 %all_to_all.25.stat_ref = f32[8,8,128]{2,1,0:T(8,128)S(1)} all-to-all(f32[8,8,128]{2,1,0:T(8,128)S(1)} %get-tuple-element.48), channel_id=1, replica_groups=mesh['dp'=2,'seq'=16,'head'=8] {'head'}, dimensions={0} | all-to-all | bytes 65536 | tf_op jit(solution)/shard_map/all_to_all | solution.py:412
  54.7 2.5 %output_grad.1 = (bf16[512,1024]{1,0:T(8,128)(2,1)}, f32[512,1024]{1,0:T(8,128)}, f32[16,72,128]{2,1,0:T(8,128)}, f32[4,128]{1,0:T(4,128)S(1)}) custom-call(f32[8,128]{1,0:T(8,128)S(1)} %get-tuple-element.39.rates_ref.rates, f32[8,8,128]{2,1,0:T(8,128)S(1)} %all_to_all.25.stat_ref, bf16[512,1024]{1,0:T(8,128)(2,1)S(1)} %get-tuple-element.49.q, ...), custom_call_target="tpu_custom_call" | custom-call | tf_op jit(solution)/shard_map/output_grad/pallas_call | solution.py:415
  57.2 4.8 %all-to-all-start.3 = ((f32[16,72,128]{2,1,0:T(8,128)}), f32[16,72,128]{2,1,0:T(8,128)S(1)}, u32[]{:S(2)}, u32[]{:S(2)}) async-start(f32[16,72,128]{2,1,0:T(8,128)} %get-tuple-element.52), calls=%async_computation.3 | async-start | bytes 1179648 | tf_op jit(solution)/shard_map/all_to_all | solution.py:353
  62.1 6.1 %query_grads.1 = (bf16[1,512,1024]{2,1,0:T(8,128)(2,1)}, bf16[1,512,1024]{2,1,0:T(8,128)(2,1)}) custom-call(f32[8,128]{1,0:T(8,128)S(1)} %get-tuple-element.39.rates_ref.rates, bf16[1,512,1024]{2,1,0:T(8,128)(2,1)} %k_hbm.3, bf16[1,512,1024]{2,1,0:T(8,128)(2,1)} %v_hbm.3, bf16[512,1024]{1,0:T(8,128)(2,1)} %get-tuple-element.53.g_ref, ...), custom_call_target="tpu_custom_call" | custom-call | tf_op jit(solution)/shard_map/query_grads/pallas_call | solution.py:429
  68.2 3.1 %all-to-all-done.3.x_ref = f32[16,72,128]{2,1,0:T(8,128)S(1)} async-done(((f32[16,72,128]{2,1,0:T(8,128)}), f32[16,72,128]{2,1,0:T(8,128)S(1)}, u32[]{:S(2)}, u32[]{:S(2)}) %all-to-all-start.3) | async-done | bytes 589856 | tf_op jit(solution)/shard_map/all_to_all | solution.py:353
  71.3 0.8 suffix.1
  72.1 4.8 %all-to-all-start.4 = ((f32[16,64,128]{2,1,0:T(8,128)}), f32[16,64,128]{2,1,0:T(8,128)S(1)}, u32[]{:S(2)}, u32[]{:S(2)}) async-start(f32[16,64,128]{2,1,0:T(8,128)} %get-tuple-element.61), calls=%async_computation.4 | async-start | bytes 1048576 | tf_op jit(solution)/shard_map/all_to_all | solution.py:353
  77.0 5.9 %key_value_grads.1 = (bf16[512,1024]{1,0:T(8,128)(2,1)S(1)}, bf16[512,1024]{1,0:T(8,128)(2,1)S(1)}, bf16[512,256]{1,0:T(8,128)(2,1)S(1)}, bf16[512,256]{1,0:T(8,128)(2,1)S(1)}) custom-call(f32[8,128]{1,0:T(8,128)S(1)} %get-tuple-element.39.rates_ref.rates, bf16[1,512,1024]{2,1,0:T(8,128)(2,1)} %q_ref.3, bf16[1,512,1024]{2,1,0:T(8,128)(2,1)} %k_hbm.3, ...), custom_call_target="tpu_custom_call" | custom-call | tf_op jit(solution)/shard_map/key_value_grads/pallas_call | solution.py:444
  82.9 0.1 collective-permute-start
  83.0 1.2 %collective-permute-done.other_ref = f32[8,128]{1,0:T(8,128)S(1)} collective-permute-done((f32[8,128]{1,0:T(8,128)S(1)}, f32[8,128]{1,0:T(8,128)S(1)}, u32[]{:S(2)}, u32[]{:S(2)}) %collective-permute-start) | collective-permute-done | bytes 4128 | tf_op jit(solution)/shard_map/ppermute | solution.py:455
  84.1 1.7 %all-to-all-done.4.r_ref = f32[16,64,128]{2,1,0:T(8,128)S(1)} async-done(((f32[16,64,128]{2,1,0:T(8,128)}), f32[16,64,128]{2,1,0:T(8,128)S(1)}, u32[]{:S(2)}, u32[]{:S(2)}) %all-to-all-start.4) | async-done | bytes 524320 | tf_op jit(solution)/shard_map/all_to_all | solution.py:353
  85.8 3.3 %final_grads.1 = (bf16[1,512,1024]{2,1,0:T(8,128)(2,1)}, bf16[1,512,1024]{2,1,0:T(8,128)(2,1)}, f32[8,128]{1,0:T(8,128)}) custom-call(f32[8,128]{1,0:T(8,128)S(1)} %get-tuple-element.39.rates_ref.rates, f32[16,64,128]{2,1,0:T(8,128)S(1)} %all-to-all-done.4.r_ref, bf16[1,512,1024]{2,1,0:T(8,128)(2,1)} %k_hbm.3, bf16[1,512,1024]{2,1,0:T(8,128)(2,1)} %v_hbm.3, ...), custom_call_target="tpu_custom_call" | custom-call | tf_op jit(solution)/shard_map/final_grads/pallas_call | solution.py:456
  (2 shorter events, 0.0 us)
Async XLA Ops:
  3.6 23.4 %copy-start.1 = (s32[1,512]{1,0:T(1,128)S(1)}, s32[1,512]{1,0:T(1,128)}, u32[]{:S(2)}) copy-start(s32[1,512]{1,0:T(1,128)} %mask_ref.1) | copy-start | bytes 6148
  3.6 23.4 %copy-start.2 = (f32[1,512]{1,0:T(1,128)S(1)}, f32[1,512]{1,0:T(1,128)}, u32[]{:S(2)}) copy-start(f32[1,512]{1,0:T(1,128)} %imp_ref.1) | copy-start | bytes 6148
  3.6 17.7 %all-to-all-start = ((f32[16,64,128]{2,1,0:T(8,128)}), f32[16,64,128]{2,1,0:T(8,128)S(1)}, u32[]{:S(2)}, u32[]{:S(2)}) async-start(f32[16,64,128]{2,1,0:T(8,128)} %bitcast.14), calls=%async_computation | async-start | bytes 1048576 | tf_op jit(solution)/shard_map/all_to_all | solution.py:353
  22.1 14.1 %all-to-all-start.1 = ((f32[16,64,128]{2,1,0:T(8,128)}), f32[16,64,128]{2,1,0:T(8,128)S(1)}, u32[]{:S(2)}, u32[]{:S(2)}) async-start(f32[16,64,128]{2,1,0:T(8,128)} %prefix.1), calls=%async_computation.1 | async-start | bytes 1048576 | tf_op jit(solution)/shard_map/all_to_all | solution.py:353
  26.9 9.3 %copy-start = (f32[1024]{0:T(1024)S(1)}, f32[1024]{0:T(1024)}, u32[]{:S(2)}) copy-start(f32[1024]{0:T(1024)} %param.13) | copy-start | bytes 12292
  57.2 14.1 %all-to-all-start.3 = ((f32[16,72,128]{2,1,0:T(8,128)}), f32[16,72,128]{2,1,0:T(8,128)S(1)}, u32[]{:S(2)}, u32[]{:S(2)}) async-start(f32[16,72,128]{2,1,0:T(8,128)} %get-tuple-element.52), calls=%async_computation.3 | async-start | bytes 1179648 | tf_op jit(solution)/shard_map/all_to_all | solution.py:353
  72.1 13.7 %all-to-all-start.4 = ((f32[16,64,128]{2,1,0:T(8,128)}), f32[16,64,128]{2,1,0:T(8,128)S(1)}, u32[]{:S(2)}, u32[]{:S(2)}) async-start(f32[16,64,128]{2,1,0:T(8,128)} %get-tuple-element.61), calls=%async_computation.4 | async-start | bytes 1048576 | tf_op jit(solution)/shard_map/all_to_all | solution.py:353
  82.9 1.3 %collective-permute-start = (f32[8,128]{1,0:T(8,128)S(1)}, f32[8,128]{1,0:T(8,128)S(1)}, u32[]{:S(2)}, u32[]{:S(2)}) collective-permute-start(f32[8,128]{1,0:T(8,128)S(1)} %get-tuple-element.69.own_ref), channel_id=1, source_target_pairs={{0,128},{128,0},{1,129},{129,1},{2,130},{130,2},{3,131},{131,3},{4... | collective-permute-start | bytes 12296 | tf_op jit(solution)/shard_map/ppermute | solution.py:455
